TPU v7x, 32 devices: a whole 2x2x4 slice. The times are simulated.
32 devices in a mesh: seq: 2 (over core), batch: 16 (over z, y, x).
Axes of the slice: x: 2, y: 2, z: 4, core: 2. Of those that a mesh axis runs over, the one named last changes fastest.
Arguments:
- tokens: bfloat16 [32, 1024, 768], P('batch', 'seq'), may hold values from -6 to 6
- grad_out: bfloat16 [32, 1024, 768], P('batch', 'seq'), may hold values from -6 to 6
- lengths: int32 [32], P('batch'), may hold values from 64 to 1024, as said below
- owners: int32 [288], replicated, may hold values from 0 to 31, as said below
- weight_slots: float32 [320, 32, 768], P(('seq', 'batch')), may hold values from -1 to 1
- first_slots: float32 [320, 32, 768], P(('seq', 'batch')), may hold values from -48.223551 to 48.223551
- second_slots: float32 [320, 32, 768], P(('seq', 'batch')), may hold values from 0.16384 to 94.37184
- small_params: float32 [12, 768], replicated, may hold values from -0.4 to 1.4
- small_first: float32 [12, 768], replicated, may hold values from -96 to 96
- small_second: float32 [12, 768], replicated, may hold values from 9.8304 to 163.84
- step_count: int32 [1], replicated, may hold values from 2 to 7
Outputs:
- layer_out: bfloat16 [32, 1024, 768], P('batch', 'seq')
- grad_in: float32 [32, 1024, 768], P('batch', 'seq')
- grad_slots: float32 [320, 32, 768], P(('seq', 'batch'))
- new_slots: float32 [320, 32, 768], P(('seq', 'batch'))
- new_first_slots: float32 [320, 32, 768], P(('seq', 'batch'))
- new_second_slots: float32 [320, 32, 768], P(('seq', 'batch'))
- small_grad: float32 [12, 768], replicated
- new_small: float32 [12, 768], replicated
- new_small_first: float32 [12, 768], replicated
- new_small_second: float32 [12, 768], replicated
Inputs may be any that keep to these rules, and one draw needn't show every extreme that they name: `lengths`: positions at or after a sequence's length are padding; some sequence has exactly 1024 live tokens and some exactly 64. `owners`: devices are numbered over seq and batch together, seq slowest. No device owns more than 10 panels, and some device owns exactly 10.
All inputs are finite; a program needn't handle non-finite values.
Results may differ from a plain program's by a relative error of at most 0.012.
Values may be sent and summed in bfloat16 or wider, within the bound.
No kernel may reach another device: no remote copies, remote signals or barrier semaphores. Data moves between devices by JAX's collectives and lax.ppermute only.
A program may use at most 192 MiB of HBM per device.

v0:
```python
from functools import partial
import math

import jax
import jax.numpy as jnp
import numpy as np
from jax import lax
from jax.experimental import pallas as pl
from jax.experimental.pallas import tpu as pltpu
from jax.sharding import PartitionSpec as P

beta_first = 0.9
beta_second = 0.999
adam_eps = 1e-08
learn_rate = 0.2
decay_rate = 0.01
SWAP = ((0, 1), (1, 0))

HEAD_DIM = 64
PANEL = 32
norm_eps = 1e-06
masked_score = -30.0
LANES = 128
BF = jnp.bfloat16
F32 = jnp.float32
ANY = pl.BlockSpec(memory_space=pl.ANY)


def mm(a, b):
    return lax.dot_general(a, b, (((1,), (0,)), ((), ())), preferred_element_type=F32)


def mm_nt(a, b):
    return lax.dot_general(a, b, (((1,), (1,)), ((), ())), preferred_element_type=F32)


def mm_tn(a, b):
    return lax.dot_general(a, b, (((0,), (0,)), ((), ())), preferred_element_type=F32)


def normalize(z):
    centre = z - jnp.mean(z, axis=-1, keepdims=True)
    rstd = lax.rsqrt(jnp.mean(centre * centre, axis=-1, keepdims=True) + norm_eps)
    return centre * rstd, rstd


def norm_back(zh, rstd, t):
    mean_t = jnp.mean(t, axis=-1, keepdims=True)
    mean_tz = jnp.mean(t * zh, axis=-1, keepdims=True)
    return (t - mean_t - zh * mean_tz) * rstd


def lane_half(shape, half):
    lane = lax.broadcasted_iota(jnp.int32, shape, len(shape) - 1)
    return (lane < HEAD_DIM) if half == 0 else (lane >= HEAD_DIM)


def rows_of(panels, start, count):
    return panels[start // PANEL:(start + count) // PANEL].reshape(count, panels.shape[-1])


def fetch_panels(slots, first, target, place, sem):
    def one(i, carry):
        pltpu.make_async_copy(slots.at[place[first + i]], target.at[i], sem).start()
        return carry
    lax.fori_loop(0, target.shape[0], one, 0)


def fetch_wait(slots, target, sem):
    pltpu.make_async_copy(slots.at[pl.ds(0, target.shape[0])], target, sem).wait()


def send_panels(stage, first, mine, theirs, back, sem):
    half = mine.shape[0]

    def one(i, carry):
        slot = back[first + i]

        @pl.when(slot < half)
        def _():
            pltpu.make_async_copy(stage.at[i], mine.at[slot], sem).start()

        @pl.when(slot >= half)
        def _():
            pltpu.make_async_copy(stage.at[i], theirs.at[slot - half], sem).start()

        return carry

    lax.fori_loop(0, stage.shape[0], one, 0)


def send_wait(stage, mine, sem):
    pltpu.make_async_copy(stage, mine.at[pl.ds(0, stage.shape[0])], sem).wait()


def attn_fwd_kernel(limits, place, x_ref, slots_ref, small_ref, q_ref, k_ref, v_ref, c_ref, p_ref,
                    mixed_ref, zh_ref, rstd_ref, w_ref, w_sem):
    step = pl.program_id(0)
    groups = x_ref.shape[-1] // LANES // PAIRS_FWD
    seq, group = step // groups, step % groups
    d = x_ref.shape[-1]
    block = x_ref.shape[1]

    @pl.when(step == 0)
    def _():
        fetch_panels(slots_ref, 0, w_ref, place, w_sem)
        fetch_wait(slots_ref, w_ref, w_sem)

    @pl.when(group == 0)
    def _():
        x = x_ref[0]
        q = mm(x, rows_of(w_ref, 0, d)) + small_ref[4:5, :]
        q_ref[0] = (q.astype(BF).astype(F32) * 0.125).astype(BF)
        k_ref[0] = mm(x, rows_of(w_ref, d, d)).astype(BF)
        v_ref[0] = (mm(x, rows_of(w_ref, 2 * d, d)) + small_ref[5:6, :]).astype(BF)

    limit = limits[seq]
    key = lax.broadcasted_iota(jnp.int32, (block, block), 0)
    for n in range(PAIRS_FWD):
        lanes = pl.ds(pl.multiple_of((group * PAIRS_FWD + n) * LANES, LANES), LANES)
        qp, kp, vp = q_ref[0, :, lanes], k_ref[0, :, lanes], v_ref[0, :, lanes]
        vt = vp.T
        parts = []
        for half in range(2):
            km = jnp.where(lane_half(kp.shape, half), kp, jnp.zeros_like(kp))
            s = mm_nt(km, qp)
            s = jnp.where(key < limit, s, masked_score)
            top = jnp.max(s, axis=0, keepdims=True)
            e = jnp.exp(s - top)
            total = jnp.sum(e, axis=0, keepdims=True)
            p = (e * (1.0 / total)).astype(BF)
            p_ref[2 * n + half] = p
            parts.append(mm(vt[half * HEAD_DIM:(half + 1) * HEAD_DIM], p))
        ctx_t = jnp.concatenate(parts, axis=0)
        c_ref[0, :, lanes] = ctx_t.T.astype(BF)

    @pl.when(group == groups - 1)
    def _():
        u = x_ref[0].astype(F32) + mm(c_ref[0], rows_of(w_ref, 3 * d, d)) + small_ref[6:7, :]
        zh, rstd = normalize(u)
        zh_ref[0] = zh
        rstd_ref[0] = rstd
        mixed_ref[0] = (zh * small_ref[0:1, :] + small_ref[1:2, :]).astype(BF)


def attn_fwd(x, gathered, small, limits, place):
    seqs, block, d = x.shape
    pairs = d // LANES
    groups = pairs // PAIRS_FWD
    by_seq = lambda shape: pl.BlockSpec((1,) + shape, lambda i, lim, pr: (i // groups, 0, 0))
    whole = lambda a: pl.BlockSpec(a, lambda i, lim, pr: (0, 0), pipeline_mode=pl.Buffered(1))
    act = jax.ShapeDtypeStruct((seqs, block, d), BF)
    return pl.pallas_call(
        attn_fwd_kernel,
        grid_spec=pltpu.PrefetchScalarGridSpec(
            num_scalar_prefetch=2,
            grid=(seqs * groups,),
            in_specs=[by_seq((block, d)), ANY, whole(small.shape)],
            out_specs=[by_seq((block, d))] * 4
            + [pl.BlockSpec((2 * PAIRS_FWD, block, block), lambda i, lim, pr: (i, 0, 0))]
            + [by_seq((block, d)), by_seq((block, d)), by_seq((block, 1))],
            scratch_shapes=[pltpu.VMEM((4 * d // PANEL, PANEL, d), BF), pltpu.SemaphoreType.DMA],
        ),
        out_shape=[act, act, act, act,
                   jax.ShapeDtypeStruct((seqs * 2 * pairs, block, block), BF),
                   act,
                   jax.ShapeDtypeStruct((seqs, block, d), F32),
                   jax.ShapeDtypeStruct((seqs, block, 1), F32)],
        compiler_params=pltpu.CompilerParams(vmem_limit_bytes=56 << 20, dimension_semantics=("arbitrary",)),
        name="attn_fwd",
    )(limits, place, x, gathered, small)


ROWS = 512
PAIRS_FWD = 2
PAIRS_BWD = 1
CHUNK = 1024


def ffn_kernel(place, back, mixed_ref, go_ref, w_hbm, small_ref, bh_ref,
               out_ref, dmixed_ref, sums_ref, dbh_ref, mine, theirs,
               w1, w2, hid, gp, acc, df, dyb, stage, w_sem, s_sem):
    d = mixed_ref.shape[-1]
    tokens = mixed_ref.shape[0]
    ff = bh_ref.shape[1]
    chunks = ff // CHUNK
    tiles = tokens // ROWS
    panels = CHUNK // PANEL
    first1 = 4 * d // PANEL
    first2 = first1 + ff // PANEL

    def start(c, carry):
        fetch_panels(w_hbm, first1 + c * panels, w1.at[c], place, w_sem.at[0, c])
        fetch_panels(w_hbm, first2 + c * panels, w2.at[c], place, w_sem.at[1, c])
        return carry

    lax.fori_loop(0, chunks, start, 0)

    def up(c, carry):
        fetch_wait(w_hbm, w1.at[c], w_sem.at[0, c])
        fetch_wait(w_hbm, w2.at[c], w_sem.at[1, c])
        cols = pl.ds(pl.multiple_of(c * CHUNK, CHUNK), CHUNK)
        w1c, w2c = w1[c].reshape(CHUNK, d), w2[c].reshape(CHUNK, d)
        bias = bh_ref[0:1, cols]
        for r in range(tiles):
            rows = pl.ds(r * ROWS, ROWS)
            f = mm_nt(mixed_ref[rows, :], w1c) + bias
            half_erf = 0.5 * lax.erf(f * (1.0 / math.sqrt(2.0))) + 0.5
            h = (f * half_erf).astype(BF)
            hid[rows, cols] = h
            gp[rows, cols] = (half_erf + f * (jnp.exp(-0.5 * f * f) * (1.0 / math.sqrt(2.0 * math.pi)))).astype(BF)
            part = mm(h, w2c)
            acc[rows, :] = jnp.where(c == 0, part, acc[rows, :] + part)
        return carry

    lax.fori_loop(0, chunks, up, 0)

    sums_ref[...] = jnp.zeros_like(sums_ref)

    def middle(r, carry):
        rows = pl.ds(pl.multiple_of(r * ROWS, ROWS), ROWS)
        rr = mixed_ref[rows, :].astype(F32) + acc[rows, :] + small_ref[7:8, :]
        zh, rstd = normalize(rr)
        out_ref[rows, :] = (zh * small_ref[2:3, :] + small_ref[3:4, :]).astype(BF)
        e = go_ref[rows, :].astype(F32)
        dr = norm_back(zh, rstd, e * small_ref[2:3, :])
        dy = dr.astype(BF)
        dyb[rows, :] = dy
        acc[rows, :] = dr
        sums_ref[0:1, :] += jnp.sum(e * zh, axis=0, keepdims=True)
        sums_ref[1:2, :] += jnp.sum(e, axis=0, keepdims=True)
        sums_ref[2:3, :] += jnp.sum(dy.astype(F32), axis=0, keepdims=True)
        return carry

    lax.fori_loop(0, tiles, middle, 0)

    def down(c, carry):
        cols = pl.ds(pl.multiple_of(c * CHUNK, CHUNK), CHUNK)
        w1c, w2c = w1[c].reshape(CHUNK, d), w2[c].reshape(CHUNK, d)
        dbh = jnp.zeros((1, CHUNK), F32)
        for r in range(tiles):
            rows = pl.ds(r * ROWS, ROWS)
            dfr = (mm_nt(dyb[rows, :], w2c) * gp[rows, cols].astype(F32)).astype(BF)
            df[rows, :] = dfr
            dbh += jnp.sum(dfr.astype(F32), axis=0, keepdims=True)
            acc[rows, :] += mm(dfr, w1c)
        dbh_ref[0:1, cols] = dbh

        @pl.when(c > 0)
        def _():
            send_wait(stage.at[0], mine, s_sem.at[0])
            send_wait(stage.at[1], mine, s_sem.at[1])

        stage[0] = mm_tn(df[...], mixed_ref[...]).astype(BF).reshape(panels, PANEL, d)
        send_panels(stage.at[0], first1 + c * panels, mine, theirs, back, s_sem.at[0])
        stage[1] = mm_tn(hid[:, cols], dyb[...]).astype(BF).reshape(panels, PANEL, d)
        send_panels(stage.at[1], first2 + c * panels, mine, theirs, back, s_sem.at[1])
        return carry

    lax.fori_loop(0, chunks, down, 0)
    dmixed_ref[...] = acc[...].astype(BF)
    send_wait(stage.at[0], mine, s_sem.at[0])
    send_wait(stage.at[1], mine, s_sem.at[1])


def ffn(mixed, go, gathered, small, bh, place, back, half):
    tokens, d = mixed.shape
    ff = bh.shape[1]
    full = lambda shape: pl.BlockSpec(shape, lambda i, pr, bk: (0,) * len(shape))
    return pl.pallas_call(
        ffn_kernel,
        grid_spec=pltpu.PrefetchScalarGridSpec(
            num_scalar_prefetch=2,
            grid=(1,),
            in_specs=[full((tokens, d)), full((tokens, d)), ANY,
                      full(small.shape), full(bh.shape)],
            out_specs=[full((tokens, d)), full((tokens, d)), full((8, d)), full((1, ff)),
                       ANY, ANY],
            scratch_shapes=[
                pltpu.VMEM((ff // CHUNK, CHUNK // PANEL, PANEL, d), BF),
                pltpu.VMEM((ff // CHUNK, CHUNK // PANEL, PANEL, d), BF),
                pltpu.VMEM((tokens, ff), BF), pltpu.VMEM((tokens, ff), BF),
                pltpu.VMEM((tokens, d), F32), pltpu.VMEM((tokens, CHUNK), BF),
                pltpu.VMEM((tokens, d), BF), pltpu.VMEM((2, CHUNK // PANEL, PANEL, d), BF),
                pltpu.SemaphoreType.DMA((2, ff // CHUNK)), pltpu.SemaphoreType.DMA((2,)),
            ],
        ),
        out_shape=[jax.ShapeDtypeStruct((tokens, d), BF), jax.ShapeDtypeStruct((tokens, d), BF),
                   jax.ShapeDtypeStruct((8, d), F32), jax.ShapeDtypeStruct((1, ff), F32),
                   jax.ShapeDtypeStruct((half, PANEL, d), BF), jax.ShapeDtypeStruct((half, PANEL, d), BF)],
        compiler_params=pltpu.CompilerParams(vmem_limit_bytes=60 << 20, dimension_semantics=("arbitrary",)),
        name="ffn",
    )(place, back, mixed, go, gathered, small, bh)


def attn_bwd_kernel(limits, place, back, dmixed_ref, zh_ref, rstd_ref, x_ref, q_ref, k_ref, v_ref,
                    c_ref, p_ref, w_hbm, small_ref, mine_in, theirs_in,
                    gin_ref, sums_ref, mine, theirs,
                    dctx, dq, dk, dv, dw, stage, w_ref, s_sem, w_sem):
    step = pl.program_id(0)
    groups = x_ref.shape[-1] // LANES // PAIRS_BWD
    seq, group = step // groups, step % groups
    d = x_ref.shape[-1]
    block = x_ref.shape[1]
    tiles = block // ROWS

    @pl.when(step == 0)
    def _():
        fetch_panels(w_hbm, 0, w_ref, place, w_sem)
        dw[...] = jnp.zeros_like(dw)
        sums_ref[...] = jnp.zeros_like(sums_ref)
        fetch_wait(w_hbm, w_ref, w_sem)

    @pl.when(group == 0)
    def _():
        for r in range(tiles):
            rows = pl.ds(r * ROWS, ROWS)
            e = dmixed_ref[0, rows, :].astype(F32)
            zh = zh_ref[0, rows, :]
            du = norm_back(zh, rstd_ref[0, rows, :], e * small_ref[0:1, :])
            da = du.astype(BF)
            gin_ref[0, rows, :] = du
            sums_ref[0:1, :] += jnp.sum(e * zh, axis=0, keepdims=True)
            sums_ref[1:2, :] += jnp.sum(e, axis=0, keepdims=True)
            sums_ref[4:5, :] += jnp.sum(da.astype(F32), axis=0, keepdims=True)
            dctx[rows, :] = mm_nt(da, rows_of(w_ref, 3 * d, d)).astype(BF)
            dw[pl.ds(3 * d, d), :] += mm_tn(c_ref[0, rows, :], da)

    limit = limits[seq]
    key = lax.broadcasted_iota(jnp.int32, (block, block), 0)
    for n in range(PAIRS_BWD):
        lanes = pl.ds(pl.multiple_of((group * PAIRS_BWD + n) * LANES, LANES), LANES)
        qp, kp, vp, dcp = q_ref[0, :, lanes], k_ref[0, :, lanes], v_ref[0, :, lanes], dctx[:, lanes]
        kt = kp.T
        prod_t = (dcp.astype(F32) * c_ref[0, :, lanes].astype(F32)).T
        dqt, dks, dvs = [], [], []
        for half in range(2):
            vm = jnp.where(lane_half(vp.shape, half), vp, jnp.zeros_like(vp))
            dp = mm_nt(vm, dcp)
            delta = jnp.sum(prod_t[half * HEAD_DIM:(half + 1) * HEAD_DIM], axis=0, keepdims=True)
            p = p_ref[2 * n + half]
            ds = jnp.where(key < limit, p.astype(F32) * (dp - delta), 0.0).astype(BF)
            dqt.append(mm(kt[half * HEAD_DIM:(half + 1) * HEAD_DIM], ds))
            dks.append(mm(ds, qp))
            dvs.append(mm(p, dcp))
        low = lane_half(qp.shape, 0)
        dq[:, lanes] = (jnp.concatenate(dqt, axis=0) * 0.125).T.astype(BF)
        dk[:, lanes] = jnp.where(low, dks[0], dks[1]).astype(BF)
        dv[:, lanes] = jnp.where(low, dvs[0], dvs[1]).astype(BF)

    @pl.when(group == groups - 1)
    def _():
        x = x_ref[0]
        gin_ref[0] += (mm_nt(dq[...], rows_of(w_ref, 0, d)) + mm_nt(dk[...], rows_of(w_ref, d, d))
                       + mm_nt(dv[...], rows_of(w_ref, 2 * d, d)))
        dw[pl.ds(0, d), :] += mm_tn(x, dq[...])
        dw[pl.ds(d, d), :] += mm_tn(x, dk[...])
        dw[pl.ds(2 * d, d), :] += mm_tn(x, dv[...])
        sums_ref[2:3, :] += jnp.sum(dq[...].astype(F32), axis=0, keepdims=True)
        sums_ref[3:4, :] += jnp.sum(dv[...].astype(F32), axis=0, keepdims=True)

    @pl.when(step == pl.num_programs(0) - 1)
    def _():
        stage[...] = dw[...].astype(BF).reshape(stage.shape)
        send_panels(stage, 0, mine, theirs, back, s_sem)
        send_wait(stage, mine, s_sem)


def attn_bwd(dmixed, zh, rstd, x, q, k, v, c, p, gathered, small, limits, place, back, mine, theirs):
    seqs, block, d = x.shape
    pairs = d // LANES
    groups = pairs // PAIRS_BWD
    by_seq = lambda shape: pl.BlockSpec((1,) + shape, lambda i, lim, pr, bk: (i // groups, 0, 0))
    whole = lambda a: pl.BlockSpec(a, lambda i, lim, pr, bk: (0, 0), pipeline_mode=pl.Buffered(1))
    return pl.pallas_call(
        attn_bwd_kernel,
        grid_spec=pltpu.PrefetchScalarGridSpec(
            num_scalar_prefetch=3,
            grid=(seqs * groups,),
            in_specs=[by_seq((block, d)), by_seq((block, d)), by_seq((block, 1))]
            + [by_seq((block, d))] * 5
            + [pl.BlockSpec((2 * PAIRS_BWD, block, block), lambda i, lim, pr, bk: (i, 0, 0)),
               ANY, whole(small.shape), ANY, ANY],
            out_specs=[by_seq((block, d)), pl.BlockSpec((8, d), lambda i, lim, pr, bk: (0, 0)),
                       ANY, ANY],
            scratch_shapes=[pltpu.VMEM((block, d), BF)] * 4
            + [pltpu.VMEM((4 * d, d), F32), pltpu.VMEM((4 * d // PANEL, PANEL, d), BF),
               pltpu.VMEM((4 * d // PANEL, PANEL, d), BF), pltpu.SemaphoreType.DMA, pltpu.SemaphoreType.DMA],
        ),
        out_shape=[jax.ShapeDtypeStruct((seqs, block, d), F32), jax.ShapeDtypeStruct((8, d), F32),
                   jax.ShapeDtypeStruct(mine.shape, BF), jax.ShapeDtypeStruct(mine.shape, BF)],
        input_output_aliases={14: 2, 15: 3},
        compiler_params=pltpu.CompilerParams(vmem_limit_bytes=60 << 20, dimension_semantics=("arbitrary",)),
        name="attn_bwd",
    )(limits, place, back, dmixed, zh, rstd, x, q, k, v, c, p, gathered, small, mine, theirs)


RING_ROUNDS = 5
LINKS = ("x", "y", "u", "d")
NEW_BLOCK = {
    (0, 0, "x"): (1, 0, 0), (0, 0, "y"): (0, 1, 0), (0, 0, "d"): (0, 0, 1),
    (0, 1, "x"): (1, 0, 1), (0, 1, "y"): (1, 1, 0), (0, 1, "d"): (0, 0, 2),
    (0, 2, "x"): (1, 0, 2), (0, 2, "y"): (0, 1, 2), (0, 2, "d"): (0, 0, 3),
    (0, 3, "x"): (1, 0, 3), (0, 3, "y"): (0, 1, 3), (0, 3, "d"): (1, 1, 2),
    (0, 4, "x"): (1, 1, 3), (0, 4, "y"): (1, 1, 1), (0, 4, "d"): (0, 1, 1),
    (1, 0, "x"): (1, 0, 1), (1, 0, "y"): (0, 1, 1), (1, 0, "u"): (0, 0, 0), (1, 0, "d"): (0, 0, 2),
    (1, 1, "x"): (1, 0, 2), (1, 1, "y"): (0, 1, 2), (1, 1, "u"): (1, 0, 0), (1, 1, "d"): (0, 0, 3),
    (1, 2, "x"): (1, 1, 2), (1, 2, "y"): (0, 1, 3), (1, 2, "u"): (0, 1, 0), (1, 2, "d"): (1, 0, 3),
    (1, 3, "x"): (1, 1, 0), (1, 3, "y"): (1, 1, 3), (1, 3, "d"): (1, 1, 1),
}
DUMMY = 16


def neighbour(chip, link):
    if link == "x":
        return chip ^ 1
    if link == "y":
        return chip ^ 2
    if link == "u":
        return chip - 4 if chip >= 4 else None
    return chip + 4 if chip < 12 else None


def received_block(chip, turn, link):
    layer = chip >> 2
    if layer < 2:
        block = NEW_BLOCK.get((layer, turn, link))
        if block is None:
            return None
        return block[2] * 4 + ((chip & 3) ^ (block[1] * 2 + block[0]))
    block = NEW_BLOCK.get((3 - layer, turn, {"u": "d", "d": "u"}.get(link, link)))
    if block is None:
        return None
    return (3 - block[2]) * 4 + ((chip & 3) ^ (block[1] * 2 + block[0]))


def build_schedule():
    moves, columns = [], []
    held = [{chip: -1} for chip in range(16)]
    for turn in range(RING_ROUNDS):
        fresh = []
        for link in LINKS:
            pairs, takes, gives, given = [], [DUMMY] * 16, [DUMMY] * 16, {}
            for chip in range(16):
                block = received_block(chip, turn, link)
                if block is None:
                    continue
                source = neighbour(chip, link)
                pairs.append((source, chip))
                takes[chip] = block
                gives[source] = block
                given[source] = held[source][block]
                fresh.append((chip, block, len(moves)))
            if not pairs:
                continue
            sources = sorted(set(given.values()))
            which = [sources.index(given.get(chip, sources[0])) for chip in range(16)]
            moves.append((turn, link, tuple(pairs), tuple(sources)))
            columns += [takes, which, gives]
        for chip, block, move in fresh:
            held[chip][block] = move
    return moves, np.array(columns, np.int32).T


MOVES, TABLE = build_schedule()


def feeders(move):
    takes = [received_block(chip, MOVES[move][0], MOVES[move][1]) for chip in range(16)]
    return feeding(takes, MOVES[move][0])


def feeding(blocks, turn):
    found = []
    for later, (after, link, pairs, _) in enumerate(MOVES):
        if after <= turn:
            continue
        chips = [
            source for source, target in pairs
            if blocks[source] is not None and received_block(target, after, link) == blocks[source]
        ]
        if chips:
            found.append((later, tuple(chips)))
    return found


def build_feeds():
    feeds, columns = [], []
    for move in range(len(MOVES) + 1):
        found = feeders(move) if move < len(MOVES) else feeding(list(range(16)), -1)
        feeds.append([(later, len(columns) + i) for i, (later, _) in enumerate(found)])
        columns += [[int(chip in chips) for chip in range(16)] for _, chips in found]
    return feeds, np.array(columns, np.int32).T


FEEDS, FEED_TABLE = build_feeds()


def both_kernel(mine, pair, out):
    out[...] = mine[...] + pair[...]


def add_cores(mine, pair):
    shape = (1,) + mine.shape[1:]
    block = pl.BlockSpec(shape, lambda i: (i, 0, 0, 0))
    return pl.pallas_call(
        both_kernel, grid=(mine.shape[0],), in_specs=[block, block], out_specs=block,
        out_shape=jax.ShapeDtypeStruct(mine.shape, BF),
        cost_estimate=pl.CostEstimate(flops=0, bytes_accessed=6 * mine.size, transcendentals=0),
        compiler_params=pltpu.CompilerParams(vmem_limit_bytes=8 << 20),
        name="add_cores",
    )(mine, pair)


def add_kernel(flags, row, feed, own, *refs):
    out, acc = refs[-2], refs[-1]

    def slot(r, carry):
        acc[...] = own[0, r].astype(F32)
        for ref, column in zip(refs[:-2], flags):
            @pl.when(feed[column] == 1)
            def _():
                acc[...] += ref[r].astype(F32)
        out[r] = acc[...].astype(out.dtype)
        return carry

    lax.fori_loop(0, out.shape[0], slot, 0)


def add_block(row, feed, block_column, sums, arrays, flags, dtype):
    slots = sums.shape[1]
    shape = sums.shape[1:]
    pieces = 2 if slots % 2 == 0 else 1
    piece = (slots // pieces,) + shape[1:]
    by_block = pl.BlockSpec((1,) + piece, lambda i, rw, fd: (rw[block_column], i, 0, 0))
    plain = pl.BlockSpec(piece, lambda i, rw, fd: (i, 0, 0))
    return pl.pallas_call(
        partial(add_kernel, tuple(flags)),
        grid_spec=pltpu.PrefetchScalarGridSpec(
            num_scalar_prefetch=2, grid=(pieces,),
            in_specs=[by_block] + [plain] * len(arrays), out_specs=plain,
            scratch_shapes=[pltpu.VMEM(piece[1:], F32)]),
        out_shape=jax.ShapeDtypeStruct(shape, dtype),
        cost_estimate=pl.CostEstimate(
            flops=0, bytes_accessed=2 * sums[0].size * (2 + len(arrays)), transcendentals=0),
        compiler_params=pltpu.CompilerParams(vmem_limit_bytes=12 << 20),
        name="add_block",
    )(row, feed, sums, *arrays)


def partners():
    size = lax.axis_size("batch")
    steps, bit = [], 1
    while bit < size:
        steps.append(("batch", tuple((i, i ^ bit) for i in range(size))))
        bit *= 2
    return steps + [("seq", SWAP)]


def reduce_slots(mine, theirs, small):
    me = lax.axis_index("batch")
    takes = jnp.asarray(TABLE)[me][0::3]
    row = jnp.concatenate([jnp.where(takes == DUMMY, 0, takes), jnp.stack([me])])
    feed = jnp.asarray(FEED_TABLE)[me]
    pair = lax.ppermute(theirs, "seq", SWAP)
    mine = mine.reshape((16, -1) + mine.shape[1:])
    sums = add_cores(mine, pair.reshape(mine.shape))
    steps = partners()
    early = small
    for step in (steps.pop(-2), steps.pop(-2)):
        early = early + lax.ppermute(early, *step)
    small = early
    before = []
    arrived, ready = {}, lax.optimization_barrier((row, early))[0]
    for turn in reversed(range(RING_ROUNDS)):
        gives = []
        now = [i for i, move in enumerate(MOVES) if move[0] == turn]
        for i in now:
            give = add_block(ready, feed, i, sums, [arrived[m] for m, _ in FEEDS[i]],
                             [column for _, column in FEEDS[i]], BF)
            gives.append(give)
            back = tuple((target, source) for source, target in MOVES[i][2])
            arrived[i] = lax.ppermute(give, "batch", back)
        late = [arrived[i] for i in before]
        ready, small, *late = lax.optimization_barrier((row, small, *late, *gives))
        arrived.update(zip(before, late))
        before = now
        if steps:
            small = small + lax.ppermute(small, *steps.pop(0))
    for step in steps:
        small = small + lax.ppermute(small, *step)
    last = FEEDS[len(MOVES)]
    total = add_block(row, feed, len(MOVES), sums, [arrived[m] for m, _ in last],
                      [column for _, column in last], F32)
    return total, small


def slot_table(owners, capacity):
    panel_index = jnp.arange(owners.shape[0], dtype=jnp.int32)
    same_owner = (owners[:, None] == owners[None, :]) & (
        panel_index[None, :] < panel_index[:, None]
    )
    rank_within = jnp.sum(same_owner.astype(jnp.int32), axis=1)
    return owners * capacity + rank_within


def adam_update(weight, first_old, second_old, grad_now, step_count):
    step_float = step_count[0].astype(jnp.float32)
    first_new = beta_first * first_old + (1.0 - beta_first) * grad_now
    second_new = beta_second * second_old + (1.0 - beta_second) * grad_now * grad_now
    first_hat = first_new / (1.0 - jnp.power(beta_first, step_float))
    second_hat = second_new / (1.0 - jnp.power(beta_second, step_float))
    weight_new = weight - learn_rate * (
        first_hat / (jnp.sqrt(second_hat) + adam_eps) + decay_rate * weight
    )
    return (weight_new, first_new, second_new)


def local(
    tokens,
    grad_out,
    lengths,
    owners,
    weight_slots,
    first_slots,
    second_slots,
    small_params,
    small_first,
    small_second,
    step_count,
):
    capacity = weight_slots.shape[0]
    block_rows, features = tokens.shape[1:]
    slot_of = slot_table(owners, capacity)
    devices = lax.axis_size("seq") * lax.axis_size("batch")
    device = lax.axis_index("seq") * lax.axis_size("batch") + lax.axis_index("batch")
    limits = lengths - lax.axis_index("seq") * block_rows
    core = lax.axis_index("seq")
    batch = lax.axis_size("batch")
    half = batch * capacity
    owner_core = (owners >= batch).astype(jnp.int32)
    back = slot_of - owner_core * half + jnp.where(owner_core == core, 0, half)
    gathered = lax.all_gather(weight_slots.astype(BF), ("seq", "batch"), axis=0, tiled=True)
    q, k, v, ctx, probs, mixed, zh, rstd = attn_fwd(tokens, gathered, small_params, limits, slot_of)
    bias_hidden = small_params[8:].reshape(1, -1)
    layer_out, d_mixed, sums_ffn, d_bias, mine, theirs = ffn(
        mixed.reshape(-1, features), grad_out.reshape(-1, features), gathered, small_params,
        bias_hidden, slot_of, back, half)
    grad_in, sums_attn, mine, theirs = attn_bwd(
        d_mixed.reshape(tokens.shape), zh, rstd, tokens, q, k, v, ctx, probs, gathered,
        small_params, limits, slot_of, back, mine, theirs)
    small_local = jnp.concatenate(
        [sums_attn[0:2], sums_ffn[0:2], sums_attn[2:5], sums_ffn[2:3],
         d_bias.reshape(-1, features)], axis=0)
    if batch == 16 and lax.axis_size("seq") == 2:
        grad_slots, small_grad = reduce_slots(mine, theirs, small_local)
    else:
        both = jnp.where(core == 0, jnp.stack([mine, theirs]), jnp.stack([theirs, mine]))
        grad_slots = lax.psum_scatter(
            both.reshape((-1,) + mine.shape[1:]), ("seq", "batch"), scatter_dimension=0,
            tiled=True).astype(jnp.float32)
        small_grad = small_local
        for step in partners():
            small_grad = small_grad + lax.ppermute(small_grad, *step)
    held = jnp.sum((owners == device).astype(jnp.int32))
    used = jnp.arange(capacity, dtype=jnp.int32) < held
    grad_slots = jnp.where(used[:, None, None], grad_slots, 0.0)
    new_slots, new_first_slots, new_second_slots = adam_update(
        weight_slots, first_slots, second_slots, grad_slots, step_count
    )
    new_small, new_small_first, new_small_second = adam_update(
        small_params, small_first, small_second, small_grad, step_count
    )
    return (
        layer_out.reshape(tokens.shape),
        grad_in,
        grad_slots,
        new_slots,
        new_first_slots,
        new_second_slots,
        small_grad,
        new_small,
        new_small_first,
        new_small_second,
    )


def solution(mesh):
    in_specs = (
        P("batch", "seq", None),
        P("batch", "seq", None),
        P("batch"),
        P(),
        P(("seq", "batch"), None, None),
        P(("seq", "batch"), None, None),
        P(("seq", "batch"), None, None),
        P(),
        P(),
        P(),
        P(),
    )
    out_specs = (
        P("batch", "seq", None),
        P("batch", "seq", None),
        P(("seq", "batch"), None, None),
        P(("seq", "batch"), None, None),
        P(("seq", "batch"), None, None),
        P(("seq", "batch"), None, None),
        P(),
        P(),
        P(),
        P(),
    )
    return jax.shard_map(local, mesh=mesh, in_specs=in_specs, out_specs=out_specs, check_vma=False)
```

profile of v0, /device:TPU:0, one launch (start us, length us, event | category | flops | bytes accessed | tf_op | source)
XLA Modules:
  0.0 363.2 jit_solution(9768914305000290259)
XLA Ops:
  7.2 2.0 convert_element_type.19
  12.9 1.9 select_add_fusion
  14.8 109.5 %all-gather.2.cloned.1.call-done.slots_ref.w_hbm = bf16[320,32,768]{2,1,0:T(8,128)(2,1)} async-done(((bf16[10,32,768]{2,1,0:T(8,128)(2,1)}), bf16[320,32,768]{2,1,0:T(8,128)(2,1)}) %all-gather.2.cloned.1.call-update) | async-done | bytes 15728656 | tf_op jit(solution)/shard_map/all_gather | solution.py:643
  124.3 29.9 %attn_fwd.1 = (bf16[2,512,768]{2,1,0:T(8,128)(2,1)}, bf16[2,512,768]{2,1,0:T(8,128)(2,1)}, bf16[2,512,768]{2,1,0:T(8,128)(2,1)}, bf16[2,512,768]{2,1,0:T(8,128)(...) custom-call(s32[2]{0:T(128)} %broadcast_subtract_fusion.limits, ...), custom_call_target="tpu_custom_call" | custom-call | tf_op jit(solution)/shard_map/attn_fwd/pallas_call | solution.py:153
  154.2 49.1 %ffn.1 = (bf16[1024,768]{1,0:T(8,128)(2,1)}, bf16[1024,768]{1,0:T(8,128)(2,1)}, f32[8,768]{1,0:T(8,128)}, f32[1,3072]{1,0:T(1,128)}, bf16[160,32,768]{2,1,0:T(8,128)(2,1)}, /*index=5*/bf16[160,32,768]{2,1,0:T(8,128)(2,1)}) custom-call(s32[288]{0:T(512)} %get-tuple-element.84.place, s32[288]{0:T(512)} %get-tuple-element.83.back, bf16[1024,768]{1,0:T(8,128)(2,1)} %bitcast.20, ...), custom_call_target="tpu_custom_call" | custom-call | tf_op jit(solution)/shard_map/ffn/pallas_call | solution.py:270
  203.4 39.8 %attn_bwd.1 = (f32[2,512,768]{2,1,0:T(8,128)}, f32[8,768]{1,0:T(8,128)}, bf16[160,32,768]{2,1,0:T(8,128)(2,1)}, bf16[160,32,768]{2,1,0:T(8,128)(2,1)}) custom-call(s32[2]{0:T(128)} %broadcast_subtract_fusion.limits, s32[288]{0:T(512)} %get-tuple-element.84.place, s32[288]{0:T(512)} %get-tuple-element.83.back, ...), custom_call_target="tpu_custom_call", output_to_operand_aliasing={{2}: (14, {}), {3}: (15, {})} | custom-call | tf_op jit(solution)/shard_map/attn_bwd/pallas_call | solution.py:375
  248.5 1.6 collective-permute-start.1
  250.8 3.6 collective-permute-done.1
  254.5 4.0 %collective-permute-done.2 = f32[12,768]{1,0:T(8,128)S(1)} collective-permute-done((f32[12,768]{1,0:T(8,128)S(1)}, f32[12,768]{1,0:T(8,128)S(1)}, u32[]{:S(2)}, u32[]{:S(2)}) %collective-permute-start.2) | collective-permute-done | bytes 36896 | tf_op jit(solution)/shard_map/ppermute | solution.py:571
  258.5 3.2 copy-done
  261.8 9.3 %add_cores.1.own = bf16[16,10,32,768]{3,2,1,0:T(8,128)(2,1)S(1)} custom-call(bf16[16,10,32,768]{3,2,1,0:T(8,128)(2,1)S(1)} %bitcast.17, bf16[16,10,32,768]{3,2,1,0:T(8,128)(2,1)} %bitcast.8.pair), custom_call_target="tpu_custom_call" | custom-call | bytes 23592960 | tf_op jit(solution)/shard_map/add_cores/pallas_call | solution.py:506
  271.8 3.3 collective-permute-start.4
  275.8 1.3 collective-permute-start.7
  279.8 3.4 collective-permute-start.5
  285.1 1.5 collective-permute-done.3
  289.5 1.5 collective-permute-start.9
  291.6 3.2 collective-permute-done.5.refs_0_
  295.4 1.6 collective-permute-done.12.refs_1_
  300.0 3.0 collective-permute-done.9.refs_0_
  303.0 2.4 collective-permute-done.10.refs_1_
  306.3 1.3 collective-permute-start.17
  309.8 2.4 collective-permute-start.8
  312.2 3.0 collective-permute-done.8
  316.8 1.5 collective-permute-start.18
  319.9 4.2 %collective-permute-start.20 = (bf16[10,32,768]{2,1,0:T(8,128)(2,1)S(1)}, bf16[10,32,768]{2,1,0:T(8,128)(2,1)S(1)}, u32[]{:S(2)}, u32[]{:S(2)}) collective-permute-start(bf16[10,32,768]{2,1,0:T(8,128)(2,1)S(1)} %add_block.36), channel_id=1, source_target_pairs={{0,4},{1,5},{2,6},{3,7},{4,8},{5,9},{6,10},{7,11},{8,12},{9,13},{1... | collective-permute-start | bytes 1474568 | tf_op jit(solution)/shard_map/ppermute | solution.py:583
  328.8 2.0 collective-permute-start.22
  331.8 4.7 %collective-permute-start.25 = (bf16[10,32,768]{2,1,0:T(8,128)(2,1)S(1)}, bf16[10,32,768]{2,1,0:T(8,128)(2,1)S(1)}, u32[]{:S(2)}, u32[]{:S(2)}) collective-permute-start(bf16[10,32,768]{2,1,0:T(8,128)(2,1)S(1)} %add_block.40), channel_id=1, source_target_pairs={{0,4},{1,5},{2,6},{3,7},{4,8},{5,9},{6,10},{7,11},{8,12},{9,13},{1... | collective-permute-start | bytes 1474568 | tf_op jit(solution)/shard_map/ppermute | solution.py:583
  337.5 1.4 collective-permute-start.24
  340.0 1.6 collective-permute-start.21
  343.7 3.3 collective-permute-done.25.refs_3_
  347.0 5.3 %collective-permute-done.24.refs_2_ = bf16[10,32,768]{2,1,0:T(8,128)(2,1)S(1)} collective-permute-done((bf16[10,32,768]{2,1,0:T(8,128)(2,1)S(1)}, bf16[10,32,768]{2,1,0:T(8,128)(2,1)S(1)}, u32[]{:S(2)}, u32[]{:S(2)}) %collective-permute-start.24) | collective-permute-done | bytes 491552 | tf_op jit(solution)/shard_map/ppermute | solution.py:583
  354.0 2.3 multiply_subtract_fusion
  (93 shorter events, 39.9 us)
Async XLA Ops:
  7.2 117.1 %all-gather.2.cloned.1.call-start = ((), (), s32[]{:S(2)}) async-start(), calls=%async_computation | async-start | bytes 16220160 | tf_op jit(solution)/shard_map/all_gather | solution.py:643
  203.3 44.5 %copy-start.8 = (f32[1,3072]{1,0:T(1,128)S(1)}, f32[1,3072]{1,0:T(1,128)}, u32[]{:S(2)}) copy-start(f32[1,3072]{1,0:T(1,128)} %get-tuple-element.60) | copy-start | bytes 36868
  243.2 15.4 %collective-permute-start = (bf16[160,32,768]{2,1,0:T(8,128)(2,1)}, bf16[160,32,768]{2,1,0:T(8,128)(2,1)}, u32[]{:S(2)}, u32[]{:S(2)}) collective-permute-start(bf16[160,32,768]{2,1,0:T(8,128)(2,1)} %get-tuple-element.57), channel_id=1, source_target_pairs={{0,16},{16,0},{1,17},{17,1},{2,18},{18,2},{3,19},{19,3},{4,20},{20... | collective-permute-start | bytes 23592968 | tf_op jit(solution)/shard_map/ppermute | solution.py:565
  248.5 5.8 %collective-permute-start.1 = (f32[12,768]{1,0:T(8,128)S(1)}, f32[12,768]{1,0:T(8,128)S(1)}, u32[]{:S(2)}, u32[]{:S(2)}) collective-permute-start(f32[12,768]{1,0:T(8,128)S(1)} %concatenate.7), channel_id=1, source_target_pairs={{0,8},{1,9},{2,10},{3,11},{4,12},{5,13},{6,14},{7,15},{8,0},{9,1},... | collective-permute-start | bytes 110600 | tf_op jit(solution)/shard_map/ppermute | solution.py:571
  254.4 4.1 %collective-permute-start.2 = (f32[12,768]{1,0:T(8,128)S(1)}, f32[12,768]{1,0:T(8,128)S(1)}, u32[]{:S(2)}, u32[]{:S(2)}) collective-permute-start(f32[12,768]{1,0:T(8,128)S(1)} %add.62), channel_id=1, source_target_pairs={{0,4},{1,5},{2,6},{3,7},{4,0},{5,1},{6,2},{7,3},{8,12},{9,13},{10,... | collective-permute-start | bytes 110600 | tf_op jit(solution)/shard_map/ppermute | solution.py:571
  271.8 16.2 %collective-permute-start.4 = (bf16[10,32,768]{2,1,0:T(8,128)(2,1)S(1)}, bf16[10,32,768]{2,1,0:T(8,128)(2,1)S(1)}, u32[]{:S(2)}, u32[]{:S(2)}) collective-permute-start(bf16[10,32,768]{2,1,0:T(8,128)(2,1)S(1)} %add_block.21), channel_id=1, source_target_pairs={{0,1},{1,0},{2,3},{3,2},{12,13},{13,12},{14,15},{15,14},{16,17},{1... | collective-permute-start | bytes 1474568 | tf_op jit(solution)/shard_map/ppermute | solution.py:583
  275.8 13.7 %collective-permute-start.7 = (bf16[10,32,768]{2,1,0:T(8,128)(2,1)S(1)}, bf16[10,32,768]{2,1,0:T(8,128)(2,1)S(1)}, u32[]{:S(2)}, u32[]{:S(2)}) collective-permute-start(bf16[10,32,768]{2,1,0:T(8,128)(2,1)S(1)} %add_block.24), channel_id=1, source_target_pairs={{0,4},{1,5},{2,6},{3,7},{16,20},{17,21},{18,22},{19,23}} | collective-permute-start | bytes 1474568 | tf_op jit(solution)/shard_map/ppermute | solution.py:583
  277.8 13.2 %collective-permute-start.6 = (bf16[10,32,768]{2,1,0:T(8,128)(2,1)S(1)}, bf16[10,32,768]{2,1,0:T(8,128)(2,1)S(1)}, u32[]{:S(2)}, u32[]{:S(2)}) collective-permute-start(bf16[10,32,768]{2,1,0:T(8,128)(2,1)S(1)} %add_block.23), channel_id=1, source_target_pairs={{12,8},{13,9},{14,10},{15,11},{28,24},{29,25},{30,26},{31,27}} | collective-permute-start | bytes 1474568 | tf_op jit(solution)/shard_map/ppermute | solution.py:583
  279.1 7.5 %collective-permute-start.3 = (f32[12,768]{1,0:T(8,128)S(1)}, f32[12,768]{1,0:T(8,128)S(1)}, u32[]{:S(2)}, u32[]{:S(2)}) collective-permute-start(f32[12,768]{1,0:T(8,128)S(1)} %add.63), channel_id=1, source_target_pairs={{0,1},{1,0},{2,3},{3,2},{4,5},{5,4},{6,7},{7,6},{8,9},{9,8},{10,11... | collective-permute-start | bytes 110600 | tf_op jit(solution)/shard_map/ppermute | solution.py:589
  279.8 15.0 %collective-permute-start.5 = (bf16[10,32,768]{2,1,0:T(8,128)(2,1)S(1)}, bf16[10,32,768]{2,1,0:T(8,128)(2,1)S(1)}, u32[]{:S(2)}, u32[]{:S(2)}) collective-permute-start(bf16[10,32,768]{2,1,0:T(8,128)(2,1)S(1)} %add_block.22), channel_id=1, source_target_pairs={{0,2},{1,3},{2,0},{3,1},{12,14},{13,15},{14,12},{15,13},{16,18},{1... | collective-permute-start | bytes 1474568 | tf_op jit(solution)/shard_map/ppermute | solution.py:583
  286.6 10.4 %collective-permute-start.12 = (bf16[10,32,768]{2,1,0:T(8,128)(2,1)S(1)}, bf16[10,32,768]{2,1,0:T(8,128)(2,1)S(1)}, u32[]{:S(2)}, u32[]{:S(2)}) collective-permute-start(bf16[10,32,768]{2,1,0:T(8,128)(2,1)S(1)} %add_block.28), channel_id=1, source_target_pairs={{0,4},{1,5},{2,6},{3,7},{4,8},{5,9},{6,10},{7,11},{16,20},{17,21},... | collective-permute-start | bytes 1474568 | tf_op jit(solution)/shard_map/ppermute | solution.py:583
  287.9 9.1 %collective-permute-start.11 = (bf16[10,32,768]{2,1,0:T(8,128)(2,1)S(1)}, bf16[10,32,768]{2,1,0:T(8,128)(2,1)S(1)}, u32[]{:S(2)}, u32[]{:S(2)}) collective-permute-start(bf16[10,32,768]{2,1,0:T(8,128)(2,1)S(1)} %add_block.27), channel_id=1, source_target_pairs={{8,4},{9,5},{10,6},{11,7},{12,8},{13,9},{14,10},{15,11},{24,20},{2... | collective-permute-start | bytes 1474568 | tf_op jit(solution)/shard_map/ppermute | solution.py:583
  289.5 13.4 %collective-permute-start.9 = (bf16[10,32,768]{2,1,0:T(8,128)(2,1)S(1)}, bf16[10,32,768]{2,1,0:T(8,128)(2,1)S(1)}, u32[]{:S(2)}, u32[]{:S(2)}) collective-permute-start(bf16[10,32,768]{2,1,0:T(8,128)(2,1)S(1)} %add_block.25), channel_id=1, source_target_pairs={{0,1},{1,0},{2,3},{3,2},{4,5},{5,4},{6,7},{7,6},{8,9},{9,8},{10,11... | collective-permute-start | bytes 1474568 | tf_op jit(solution)/shard_map/ppermute | solution.py:583
  291.0 14.3 %collective-permute-start.10 = (bf16[10,32,768]{2,1,0:T(8,128)(2,1)S(1)}, bf16[10,32,768]{2,1,0:T(8,128)(2,1)S(1)}, u32[]{:S(2)}, u32[]{:S(2)}) collective-permute-start(bf16[10,32,768]{2,1,0:T(8,128)(2,1)S(1)} %add_block.26), channel_id=1, source_target_pairs={{0,2},{1,3},{2,0},{3,1},{4,6},{5,7},{6,4},{7,5},{8,10},{9,11},{10,... | collective-permute-start | bytes 1474568 | tf_op jit(solution)/shard_map/ppermute | solution.py:583
  297.8 18.1 %collective-permute-start.14 = (bf16[10,32,768]{2,1,0:T(8,128)(2,1)S(1)}, bf16[10,32,768]{2,1,0:T(8,128)(2,1)S(1)}, u32[]{:S(2)}, u32[]{:S(2)}) collective-permute-start(bf16[10,32,768]{2,1,0:T(8,128)(2,1)S(1)} %add_block.29), channel_id=1, source_target_pairs={{0,1},{1,0},{2,3},{3,2},{4,5},{5,4},{6,7},{7,6},{8,9},{9,8},{10,11... | collective-permute-start | bytes 1474568 | tf_op jit(solution)/shard_map/ppermute | solution.py:583
  299.0 19.9 %collective-permute-start.15 = (bf16[10,32,768]{2,1,0:T(8,128)(2,1)S(1)}, bf16[10,32,768]{2,1,0:T(8,128)(2,1)S(1)}, u32[]{:S(2)}, u32[]{:S(2)}) collective-permute-start(bf16[10,32,768]{2,1,0:T(8,128)(2,1)S(1)} %add_block.30), channel_id=1, source_target_pairs={{0,2},{1,3},{2,0},{3,1},{4,6},{5,7},{6,4},{7,5},{8,10},{9,11},{10,... | collective-permute-start | bytes 1474568 | tf_op jit(solution)/shard_map/ppermute | solution.py:583
  306.3 12.6 %collective-permute-start.17 = (bf16[10,32,768]{2,1,0:T(8,128)(2,1)S(1)}, bf16[10,32,768]{2,1,0:T(8,128)(2,1)S(1)}, u32[]{:S(2)}, u32[]{:S(2)}) collective-permute-start(bf16[10,32,768]{2,1,0:T(8,128)(2,1)S(1)} %add_block.32), channel_id=1, source_target_pairs={{0,4},{1,5},{2,6},{3,7},{4,8},{5,9},{6,10},{7,11},{8,12},{9,13},{1... | collective-permute-start | bytes 1474568 | tf_op jit(solution)/shard_map/ppermute | solution.py:583
  308.5 15.6 %collective-permute-start.16 = (bf16[10,32,768]{2,1,0:T(8,128)(2,1)S(1)}, bf16[10,32,768]{2,1,0:T(8,128)(2,1)S(1)}, u32[]{:S(2)}, u32[]{:S(2)}) collective-permute-start(bf16[10,32,768]{2,1,0:T(8,128)(2,1)S(1)} %add_block.31), channel_id=1, source_target_pairs={{4,0},{5,1},{6,2},{7,3},{8,4},{9,5},{10,6},{11,7},{12,8},{13,9},{1... | collective-permute-start | bytes 1474568 | tf_op jit(solution)/shard_map/ppermute | solution.py:583
  309.8 5.3 %collective-permute-start.8 = (f32[12,768]{1,0:T(8,128)S(1)}, f32[12,768]{1,0:T(8,128)S(1)}, u32[]{:S(2)}, u32[]{:S(2)}) collective-permute-start(f32[12,768]{1,0:T(8,128)S(1)} %add.64), channel_id=1, source_target_pairs={{0,2},{1,3},{2,0},{3,1},{4,6},{5,7},{6,4},{7,5},{8,10},{9,11},{10,... | collective-permute-start | bytes 110600 | tf_op jit(solution)/shard_map/ppermute | solution.py:589
  316.8 14.0 %collective-permute-start.18 = (bf16[10,32,768]{2,1,0:T(8,128)(2,1)S(1)}, bf16[10,32,768]{2,1,0:T(8,128)(2,1)S(1)}, u32[]{:S(2)}, u32[]{:S(2)}) collective-permute-start(bf16[10,32,768]{2,1,0:T(8,128)(2,1)S(1)} %add_block.34), channel_id=1, source_target_pairs={{0,2},{1,3},{2,0},{3,1},{4,6},{5,7},{6,4},{7,5},{8,10},{9,11},{10,... | collective-permute-start | bytes 1474568 | tf_op jit(solution)/shard_map/ppermute | solution.py:583
  318.3 12.5 %collective-permute-start.23 = (bf16[10,32,768]{2,1,0:T(8,128)(2,1)S(1)}, bf16[10,32,768]{2,1,0:T(8,128)(2,1)S(1)}, u32[]{:S(2)}, u32[]{:S(2)}) collective-permute-start(bf16[10,32,768]{2,1,0:T(8,128)(2,1)S(1)} %add_block.33), channel_id=1, source_target_pairs={{0,1},{1,0},{2,3},{3,2},{4,5},{5,4},{6,7},{7,6},{8,9},{9,8},{10,11... | collective-permute-start | bytes 1474568 | tf_op jit(solution)/shard_map/ppermute | solution.py:583
  319.9 10.8 %collective-permute-start.20 = (bf16[10,32,768]{2,1,0:T(8,128)(2,1)S(1)}, bf16[10,32,768]{2,1,0:T(8,128)(2,1)S(1)}, u32[]{:S(2)}, u32[]{:S(2)}) collective-permute-start(bf16[10,32,768]{2,1,0:T(8,128)(2,1)S(1)} %add_block.36), channel_id=1, source_target_pairs={{0,4},{1,5},{2,6},{3,7},{4,8},{5,9},{6,10},{7,11},{8,12},{9,13},{1... | collective-permute-start | bytes 1474568 | tf_op jit(solution)/shard_map/ppermute | solution.py:583
  325.1 11.4 %collective-permute-start.19 = (bf16[10,32,768]{2,1,0:T(8,128)(2,1)S(1)}, bf16[10,32,768]{2,1,0:T(8,128)(2,1)S(1)}, u32[]{:S(2)}, u32[]{:S(2)}) collective-permute-start(bf16[10,32,768]{2,1,0:T(8,128)(2,1)S(1)} %add_block.35), channel_id=1, source_target_pairs={{4,0},{5,1},{6,2},{7,3},{8,4},{9,5},{10,6},{11,7},{12,8},{13,9},{1... | collective-permute-start | bytes 1474568 | tf_op jit(solution)/shard_map/ppermute | solution.py:583
  326.4 1.3 collective-permute-start.13
  327.7 15.3 %copy-start.5 = (f32[12,768]{1,0:T(8,128)}, f32[12,768]{1,0:T(8,128)S(1)}, u32[]{:S(2)}) copy-start(f32[12,768]{1,0:T(8,128)S(1)} %add.66) | copy-start | bytes 110596
  328.8 14.9 %collective-permute-start.22 = (bf16[10,32,768]{2,1,0:T(8,128)(2,1)S(1)}, bf16[10,32,768]{2,1,0:T(8,128)(2,1)S(1)}, u32[]{:S(2)}, u32[]{:S(2)}) collective-permute-start(bf16[10,32,768]{2,1,0:T(8,128)(2,1)S(1)} %add_block.38), channel_id=1, source_target_pairs={{0,2},{1,3},{2,0},{3,1},{4,6},{5,7},{6,4},{7,5},{8,10},{9,11},{10,... | collective-permute-start | bytes 1474568 | tf_op jit(solution)/shard_map/ppermute | solution.py:583
  331.8 15.2 %collective-permute-start.25 = (bf16[10,32,768]{2,1,0:T(8,128)(2,1)S(1)}, bf16[10,32,768]{2,1,0:T(8,128)(2,1)S(1)}, u32[]{:S(2)}, u32[]{:S(2)}) collective-permute-start(bf16[10,32,768]{2,1,0:T(8,128)(2,1)S(1)} %add_block.40), channel_id=1, source_target_pairs={{0,4},{1,5},{2,6},{3,7},{4,8},{5,9},{6,10},{7,11},{8,12},{9,13},{1... | collective-permute-start | bytes 1474568 | tf_op jit(solution)/shard_map/ppermute | solution.py:583
  337.5 14.8 %collective-permute-start.24 = (bf16[10,32,768]{2,1,0:T(8,128)(2,1)S(1)}, bf16[10,32,768]{2,1,0:T(8,128)(2,1)S(1)}, u32[]{:S(2)}, u32[]{:S(2)}) collective-permute-start(bf16[10,32,768]{2,1,0:T(8,128)(2,1)S(1)} %add_block.39), channel_id=1, source_target_pairs={{4,0},{5,1},{6,2},{7,3},{8,4},{9,5},{10,6},{11,7},{12,8},{13,9},{1... | collective-permute-start | bytes 1474568 | tf_op jit(solution)/shard_map/ppermute | solution.py:583
  340.0 12.8 %collective-permute-start.21 = (bf16[10,32,768]{2,1,0:T(8,128)(2,1)S(1)}, bf16[10,32,768]{2,1,0:T(8,128)(2,1)S(1)}, u32[]{:S(2)}, u32[]{:S(2)}) collective-permute-start(bf16[10,32,768]{2,1,0:T(8,128)(2,1)S(1)} %add_block.37), channel_id=1, source_target_pairs={{0,1},{1,0},{2,3},{3,2},{4,5},{5,4},{6,7},{7,6},{8,9},{9,8},{10,11... | collective-permute-start | bytes 1474568 | tf_op jit(solution)/shard_map/ppermute | solution.py:583
  343.6 10.3 %copy-start.1 = (f32[10,32,768]{2,1,0:T(8,128)S(1)}, f32[10,32,768]{2,1,0:T(8,128)}, u32[]{:S(2)}) copy-start(f32[10,32,768]{2,1,0:T(8,128)} %param.17) | copy-start | bytes 2949124
  343.6 10.3 %copy-start.2 = (f32[10,32,768]{2,1,0:T(8,128)S(1)}, f32[10,32,768]{2,1,0:T(8,128)}, u32[]{:S(2)}) copy-start(f32[10,32,768]{2,1,0:T(8,128)} %param.19) | copy-start | bytes 2949124
  343.6 10.3 %copy-start.3 = (f32[10,32,768]{2,1,0:T(8,128)S(1)}, f32[10,32,768]{2,1,0:T(8,128)}, u32[]{:S(2)}) copy-start(f32[10,32,768]{2,1,0:T(8,128)} %param.18) | copy-start | bytes 2949124
  (4 other events, 19.8 us)
Sparse Core Ops, SparseCore 0:
  11.5 112.7 all-gather.1
where the time goes:
time: 365 us; the launch traced here: 363 us
  Pallas kernels  146 us (40%)
  waiting for transfers between devices  142 us (39%)
  starting transfers between devices  39.9 us (11%)
  between operations  15.3 us (4%)
  other arithmetic  10.6 us (3%)
  local copies, waits for them, and re-layouts  9.64 us (3%)
    all_gather x1, waiting for transfers between devices, local(): lax.all_gather(weight_slots.astype(BF), ('seq', 'batch'), axis=0, tiled=T...  110 us
    pallas_call x1, Pallas kernels, ffn(): pl.pallas_call(ffn_kernel, grid_spec=pltpu.PrefetchScalarGridSpec(num_sca...  49.1 us
    pallas_call x1, Pallas kernels, attn_bwd(): pl.pallas_call(attn_bwd_kernel, grid_spec=pltpu.PrefetchScalarGridSpec(nu...  39.8 us
    ppermute x20, starting transfers between devices, reduce_slots(): arrived[i] = lax.ppermute(give, 'batch', back)  34.8 us
    pallas_call x1, Pallas kernels, attn_fwd(): pl.pallas_call(attn_fwd_kernel, grid_spec=pltpu.PrefetchScalarGridSpec(nu...  29.9 us
    ppermute x20, waiting for transfers between devices, reduce_slots(): arrived[i] = lax.ppermute(give, 'batch', back)  19.2 us
    pallas_call x21, Pallas kernels, add_block(): pl.pallas_call(partial(add_kernel, tuple(flags)), grid_spec=pltpu.Prefetc...  17.6 us
    pallas_call x1, Pallas kernels, add_cores(): pl.pallas_call(both_kernel, grid=(mine.shape[0],), in_specs=[block, block...  9.34 us
  transfers between devices with their start and end apart: 27, of which 13 were waited for; matrix products, arithmetic and copies ran while one was open for 3% of the time, Pallas kernels for 4%

commit v1 on v0

--- a/solution.py
+++ b/solution.py
@@ -496,18 +496,59 @@
 FEEDS, FEED_TABLE = build_feeds()
 
 
-def both_kernel(mine, pair, out):
-    out[...] = mine[...] + pair[...]
+def load_kernel(mine, out, sems):
+    def copy(i):
+        return pltpu.make_async_copy(mine.at[i], out.at[i], sems.at[i])
+
+    def start(i, carry):
+        copy(i).start()
+        return carry
+
+    def wait(i, carry):
+        copy(i).wait()
+        return carry
+
+    lax.fori_loop(0, out.shape[0], start, 0)
+    lax.fori_loop(0, out.shape[0], wait, 0)
+
+
+def load_core(mine):
+    return pl.pallas_call(
+        load_kernel, in_specs=[ANY], out_specs=pl.BlockSpec(memory_space=pltpu.VMEM),
+        out_shape=jax.ShapeDtypeStruct(mine.shape, BF),
+        scratch_shapes=[pltpu.SemaphoreType.DMA((mine.shape[0],))],
+        cost_estimate=pl.CostEstimate(flops=0, bytes_accessed=4 * mine.size, transcendentals=0),
+        compiler_params=pltpu.CompilerParams(vmem_limit_bytes=12 << 20),
+        name="load_core",
+    )(mine)
+
+
+def both_kernel(mine, pair, out, room, sems):
+    def copy(i):
+        return pltpu.make_async_copy(pair.at[i], room.at[i], sems.at[i])
+
+    def start(i, carry):
+        copy(i).start()
+        return carry
+
+    def add(i, carry):
+        copy(i).wait()
+        out[i] = mine[i] + room[i]
+        return carry
+
+    lax.fori_loop(0, out.shape[0], start, 0)
+    lax.fori_loop(0, out.shape[0], add, 0)
 
 
 def add_cores(mine, pair):
-    shape = (1,) + mine.shape[1:]
-    block = pl.BlockSpec(shape, lambda i: (i, 0, 0, 0))
+    whole = pl.BlockSpec(memory_space=pltpu.VMEM)
     return pl.pallas_call(
-        both_kernel, grid=(mine.shape[0],), in_specs=[block, block], out_specs=block,
+        both_kernel, in_specs=[whole, ANY], out_specs=whole,
         out_shape=jax.ShapeDtypeStruct(mine.shape, BF),
+        scratch_shapes=[pltpu.VMEM(mine.shape, BF), pltpu.SemaphoreType.DMA((mine.shape[0],))],
+        input_output_aliases={0: 0},
         cost_estimate=pl.CostEstimate(flops=0, bytes_accessed=6 * mine.size, transcendentals=0),
-        compiler_params=pltpu.CompilerParams(vmem_limit_bytes=8 << 20),
+        compiler_params=pltpu.CompilerParams(vmem_limit_bytes=20 << 20),
         name="add_cores",
     )(mine, pair)
 
@@ -564,7 +605,7 @@
     feed = jnp.asarray(FEED_TABLE)[me]
     pair = lax.ppermute(theirs, "seq", SWAP)
     mine = mine.reshape((16, -1) + mine.shape[1:])
-    sums = add_cores(mine, pair.reshape(mine.shape))
+    sums = add_cores(load_core(mine), pair.reshape(mine.shape))
     steps = partners()
     early = small
     for step in (steps.pop(-2), steps.pop(-2)):

time: 365 us -> 359 us (0.984)
  starting transfers between devices: 39.9 us -> 35.6 us
    ppermute x20, starting transfers between devices: 34.8 us -> 30.7 us  [reduce_slots(): arrived[i] = lax.ppermute(give, 'batch', back)]
    ppermute x2, waiting for transfers between devices: 7.57 us -> 3.52 us  [reduce_slots(): early = early + lax.ppermute(early, *step)]
    pallas_call x1 -> x2, Pallas kernels: 9.34 us -> 8.79 us  [the longest x1 5.34 us: load_core(): pl.pallas_call(load_kernel, in_specs=[ANY], out_specs=pl.BlockSpec(memory...]
  transfers between devices with their start and end apart: 27 -> 27, of which waited for: 13 -> 15; matrix products, arithmetic and copies ran while one was open for 3% -> 4% of each run, Pallas kernels for 4% -> 6%
where the time goes in v1:
time: 359 us; the launch traced here: 358 us
  Pallas kernels  144 us (40%)
  waiting for transfers between devices  142 us (40%)
  starting transfers between devices  35.6 us (10%)
  between operations  15.3 us (4%)
  other arithmetic  10.6 us (3%)
  local copies, waits for them, and re-layouts  9.65 us (3%)
    all_gather x1, waiting for transfers between devices, local(): lax.all_gather(weight_slots.astype(BF), ('seq', 'batch'), axis=0, tiled=T...  110 us
    pallas_call x1, Pallas kernels, ffn(): pl.pallas_call(ffn_kernel, grid_spec=pltpu.PrefetchScalarGridSpec(num_sca...  48.3 us
    pallas_call x1, Pallas kernels, attn_bwd(): pl.pallas_call(attn_bwd_kernel, grid_spec=pltpu.PrefetchScalarGridSpec(nu...  39.8 us
    ppermute x20, starting transfers between devices, reduce_slots(): arrived[i] = lax.ppermute(give, 'batch', back)  30.7 us
    pallas_call x1, Pallas kernels, attn_fwd(): pl.pallas_call(attn_fwd_kernel, grid_spec=pltpu.PrefetchScalarGridSpec(nu...  29.9 us
    ppermute x20, waiting for transfers between devices, reduce_slots(): arrived[i] = lax.ppermute(give, 'batch', back)  20.5 us
    pallas_call x21, Pallas kernels, add_block(): pl.pallas_call(partial(add_kernel, tuple(flags)), grid_spec=pltpu.Prefetc...  17.6 us
    ppermute x3, waiting for transfers between devices, reduce_slots(): small = small + lax.ppermute(small, *steps.pop(0))  8.41 us
  transfers between devices with their start and end apart: 27, of which 15 were waited for; matrix products, arithmetic and copies ran while one was open for 4% of the time, Pallas kernels for 6%

profile of v1, /device:TPU:0, one launch (start us, length us, event | category | flops | bytes accessed | tf_op | source)
XLA Modules:
  0.0 357.6 jit_solution(3955203783881303274)
XLA Ops:
  7.2 2.0 convert_element_type.19
  12.9 1.9 select_add_fusion
  14.8 109.5 %all-gather.2.cloned.1.call-done.slots_ref.w_hbm = bf16[320,32,768]{2,1,0:T(8,128)(2,1)} async-done(((bf16[10,32,768]{2,1,0:T(8,128)(2,1)}), bf16[320,32,768]{2,1,0:T(8,128)(2,1)}) %all-gather.2.cloned.1.call-update) | async-done | bytes 15728656 | tf_op jit(solution)/shard_map/all_gather | solution.py:684
  124.3 29.9 %attn_fwd.1 = (bf16[2,512,768]{2,1,0:T(8,128)(2,1)}, bf16[2,512,768]{2,1,0:T(8,128)(2,1)}, bf16[2,512,768]{2,1,0:T(8,128)(2,1)}, bf16[2,512,768]{2,1,0:T(8,128)(...) custom-call(s32[2]{0:T(128)} %broadcast_subtract_fusion.limits, ...), custom_call_target="tpu_custom_call" | custom-call | tf_op jit(solution)/shard_map/attn_fwd/pallas_call | solution.py:153
  154.2 48.3 %ffn.1 = (bf16[1024,768]{1,0:T(8,128)(2,1)}, bf16[1024,768]{1,0:T(8,128)(2,1)}, f32[8,768]{1,0:T(8,128)}, f32[1,3072]{1,0:T(1,128)}, bf16[160,32,768]{2,1,0:T(8,128)(2,1)}, /*index=5*/bf16[160,32,768]{2,1,0:T(8,128)(2,1)}) custom-call(s32[288]{0:T(512)} %get-tuple-element.84.place, s32[288]{0:T(512)} %get-tuple-element.83.back, bf16[1024,768]{1,0:T(8,128)(2,1)} %bitcast.20, ...), custom_call_target="tpu_custom_call" | custom-call | tf_op jit(solution)/shard_map/ffn/pallas_call | solution.py:270
  202.5 39.8 %attn_bwd.1 = (f32[2,512,768]{2,1,0:T(8,128)}, f32[8,768]{1,0:T(8,128)}, bf16[160,32,768]{2,1,0:T(8,128)(2,1)}, bf16[160,32,768]{2,1,0:T(8,128)(2,1)}) custom-call(s32[2]{0:T(128)} %broadcast_subtract_fusion.limits, s32[288]{0:T(512)} %get-tuple-element.84.place, s32[288]{0:T(512)} %get-tuple-element.83.back, ...), custom_call_target="tpu_custom_call", output_to_operand_aliasing={{2}: (14, {}), {3}: (15, {})} | custom-call | tf_op jit(solution)/shard_map/attn_bwd/pallas_call | solution.py:375
  247.8 1.6 collective-permute-start.1
  250.0 3.5 collective-permute-done.1
  253.7 3.2 copy-done
  256.9 5.3 %load_core.1.mine = bf16[16,10,32,768]{3,2,1,0:T(8,128)(2,1)S(1)} custom-call(bf16[16,10,32,768]{3,2,1,0:T(8,128)(2,1)S(1)} %bitcast.17), custom_call_target="tpu_custom_call" | custom-call | bytes 15728640 | tf_op jit(solution)/shard_map/load_core/pallas_call | solution.py:516
  262.3 3.5 add_cores.1.own
  266.4 3.3 collective-permute-start.4
  270.4 1.3 collective-permute-start.7
  273.8 1.5 collective-permute-start.3
  275.3 2.6 collective-permute-start.5
  279.8 2.6 collective-permute-done.3
  285.3 1.5 collective-permute-start.9
  287.4 3.1 collective-permute-done.5.refs_0_
  291.1 2.5 collective-permute-done.12.refs_1_
  294.4 1.5 collective-permute-start.14
  296.5 2.9 collective-permute-done.9.refs_0_
  299.4 1.6 collective-permute-done.10.refs_1_
  302.0 1.3 collective-permute-start.17
  305.4 1.4 collective-permute-start.8
  306.8 4.6 %collective-permute-done.8 = f32[12,768]{1,0:T(8,128)S(1)} collective-permute-done((f32[12,768]{1,0:T(8,128)S(1)}, f32[12,768]{1,0:T(8,128)S(1)}, u32[]{:S(2)}, u32[]{:S(2)}) %collective-permute-start.8) | collective-permute-done | bytes 36896 | tf_op jit(solution)/shard_map/ppermute | solution.py:630
  316.3 2.7 collective-permute-start.20
  325.5 1.3 collective-permute-done.20.refs_2_
  327.9 4.5 %collective-permute-start.25 = (bf16[10,32,768]{2,1,0:T(8,128)(2,1)S(1)}, bf16[10,32,768]{2,1,0:T(8,128)(2,1)S(1)}, u32[]{:S(2)}, u32[]{:S(2)}) collective-permute-start(bf16[10,32,768]{2,1,0:T(8,128)(2,1)S(1)} %add_block.40), channel_id=1, source_target_pairs={{0,4},{1,5},{2,6},{3,7},{4,8},{5,9},{6,10},{7,11},{8,12},{9,13},{1... | collective-permute-start | bytes 1474568 | tf_op jit(solution)/shard_map/ppermute | solution.py:624
  333.4 1.4 collective-permute-start.24
  338.6 2.8 collective-permute-done.25.refs_3_
  341.4 5.5 %collective-permute-done.24.refs_2_ = bf16[10,32,768]{2,1,0:T(8,128)(2,1)S(1)} collective-permute-done((bf16[10,32,768]{2,1,0:T(8,128)(2,1)S(1)}, bf16[10,32,768]{2,1,0:T(8,128)(2,1)S(1)}, u32[]{:S(2)}, u32[]{:S(2)}) %collective-permute-start.24) | collective-permute-done | bytes 491552 | tf_op jit(solution)/shard_map/ppermute | solution.py:624
  348.4 2.3 multiply_subtract_fusion
  (94 shorter events, 41.5 us)
Async XLA Ops:
  7.2 117.1 %all-gather.2.cloned.1.call-start = ((), (), s32[]{:S(2)}) async-start(), calls=%async_computation | async-start | bytes 16220160 | tf_op jit(solution)/shard_map/all_gather | solution.py:684
  202.5 44.5 %copy-start.8 = (f32[1,3072]{1,0:T(1,128)S(1)}, f32[1,3072]{1,0:T(1,128)}, u32[]{:S(2)}) copy-start(f32[1,3072]{1,0:T(1,128)} %get-tuple-element.60) | copy-start | bytes 36868
  242.4 20.0 %collective-permute-start = (bf16[160,32,768]{2,1,0:T(8,128)(2,1)}, bf16[160,32,768]{2,1,0:T(8,128)(2,1)}, u32[]{:S(2)}, u32[]{:S(2)}) collective-permute-start(bf16[160,32,768]{2,1,0:T(8,128)(2,1)} %get-tuple-element.57), channel_id=1, source_target_pairs={{0,16},{16,0},{1,17},{17,1},{2,18},{18,2},{3,19},{19,3},{4,20},{20... | collective-permute-start | bytes 23592968 | tf_op jit(solution)/shard_map/ppermute | solution.py:606
  247.8 5.8 %collective-permute-start.1 = (f32[12,768]{1,0:T(8,128)S(1)}, f32[12,768]{1,0:T(8,128)S(1)}, u32[]{:S(2)}, u32[]{:S(2)}) collective-permute-start(f32[12,768]{1,0:T(8,128)S(1)} %concatenate.7), channel_id=1, source_target_pairs={{0,8},{1,9},{2,10},{3,11},{4,12},{5,13},{6,14},{7,15},{8,0},{9,1},... | collective-permute-start | bytes 110600 | tf_op jit(solution)/shard_map/ppermute | solution.py:612
  253.5 8.7 %collective-permute-start.2 = (f32[12,768]{1,0:T(8,128)S(1)}, f32[12,768]{1,0:T(8,128)S(1)}, u32[]{:S(2)}, u32[]{:S(2)}) collective-permute-start(f32[12,768]{1,0:T(8,128)S(1)} %add.62), channel_id=1, source_target_pairs={{0,4},{1,5},{2,6},{3,7},{4,0},{5,1},{6,2},{7,3},{8,12},{9,13},{10,... | collective-permute-start | bytes 110600 | tf_op jit(solution)/shard_map/ppermute | solution.py:612
  266.4 17.3 %collective-permute-start.4 = (bf16[10,32,768]{2,1,0:T(8,128)(2,1)S(1)}, bf16[10,32,768]{2,1,0:T(8,128)(2,1)S(1)}, u32[]{:S(2)}, u32[]{:S(2)}) collective-permute-start(bf16[10,32,768]{2,1,0:T(8,128)(2,1)S(1)} %add_block.21), channel_id=1, source_target_pairs={{0,1},{1,0},{2,3},{3,2},{12,13},{13,12},{14,15},{15,14},{16,17},{1... | collective-permute-start | bytes 1474568 | tf_op jit(solution)/shard_map/ppermute | solution.py:624
  270.4 14.8 %collective-permute-start.7 = (bf16[10,32,768]{2,1,0:T(8,128)(2,1)S(1)}, bf16[10,32,768]{2,1,0:T(8,128)(2,1)S(1)}, u32[]{:S(2)}, u32[]{:S(2)}) collective-permute-start(bf16[10,32,768]{2,1,0:T(8,128)(2,1)S(1)} %add_block.24), channel_id=1, source_target_pairs={{0,4},{1,5},{2,6},{3,7},{16,20},{17,21},{18,22},{19,23}} | collective-permute-start | bytes 1474568 | tf_op jit(solution)/shard_map/ppermute | solution.py:624
  272.4 14.3 %collective-permute-start.6 = (bf16[10,32,768]{2,1,0:T(8,128)(2,1)S(1)}, bf16[10,32,768]{2,1,0:T(8,128)(2,1)S(1)}, u32[]{:S(2)}, u32[]{:S(2)}) collective-permute-start(bf16[10,32,768]{2,1,0:T(8,128)(2,1)S(1)} %add_block.23), channel_id=1, source_target_pairs={{12,8},{13,9},{14,10},{15,11},{28,24},{29,25},{30,26},{31,27}} | collective-permute-start | bytes 1474568 | tf_op jit(solution)/shard_map/ppermute | solution.py:624
  273.8 8.6 %collective-permute-start.3 = (f32[12,768]{1,0:T(8,128)S(1)}, f32[12,768]{1,0:T(8,128)S(1)}, u32[]{:S(2)}, u32[]{:S(2)}) collective-permute-start(f32[12,768]{1,0:T(8,128)S(1)} %add.63), channel_id=1, source_target_pairs={{0,1},{1,0},{2,3},{3,2},{4,5},{5,4},{6,7},{7,6},{8,9},{9,8},{10,11... | collective-permute-start | bytes 110600 | tf_op jit(solution)/shard_map/ppermute | solution.py:630
  275.3 15.2 %collective-permute-start.5 = (bf16[10,32,768]{2,1,0:T(8,128)(2,1)S(1)}, bf16[10,32,768]{2,1,0:T(8,128)(2,1)S(1)}, u32[]{:S(2)}, u32[]{:S(2)}) collective-permute-start(bf16[10,32,768]{2,1,0:T(8,128)(2,1)S(1)} %add_block.22), channel_id=1, source_target_pairs={{0,2},{1,3},{2,0},{3,1},{12,14},{13,15},{14,12},{15,13},{16,18},{1... | collective-permute-start | bytes 1474568 | tf_op jit(solution)/shard_map/ppermute | solution.py:624
  282.4 11.2 %collective-permute-start.12 = (bf16[10,32,768]{2,1,0:T(8,128)(2,1)S(1)}, bf16[10,32,768]{2,1,0:T(8,128)(2,1)S(1)}, u32[]{:S(2)}, u32[]{:S(2)}) collective-permute-start(bf16[10,32,768]{2,1,0:T(8,128)(2,1)S(1)} %add_block.28), channel_id=1, source_target_pairs={{0,4},{1,5},{2,6},{3,7},{4,8},{5,9},{6,10},{7,11},{16,20},{17,21},... | collective-permute-start | bytes 1474568 | tf_op jit(solution)/shard_map/ppermute | solution.py:624
  283.7 9.9 %collective-permute-start.11 = (bf16[10,32,768]{2,1,0:T(8,128)(2,1)S(1)}, bf16[10,32,768]{2,1,0:T(8,128)(2,1)S(1)}, u32[]{:S(2)}, u32[]{:S(2)}) collective-permute-start(bf16[10,32,768]{2,1,0:T(8,128)(2,1)S(1)} %add_block.27), channel_id=1, source_target_pairs={{8,4},{9,5},{10,6},{11,7},{12,8},{13,9},{14,10},{15,11},{24,20},{2... | collective-permute-start | bytes 1474568 | tf_op jit(solution)/shard_map/ppermute | solution.py:624
  285.3 14.1 %collective-permute-start.9 = (bf16[10,32,768]{2,1,0:T(8,128)(2,1)S(1)}, bf16[10,32,768]{2,1,0:T(8,128)(2,1)S(1)}, u32[]{:S(2)}, u32[]{:S(2)}) collective-permute-start(bf16[10,32,768]{2,1,0:T(8,128)(2,1)S(1)} %add_block.25), channel_id=1, source_target_pairs={{0,1},{1,0},{2,3},{3,2},{4,5},{5,4},{6,7},{7,6},{8,9},{9,8},{10,11... | collective-permute-start | bytes 1474568 | tf_op jit(solution)/shard_map/ppermute | solution.py:624
  286.8 14.2 %collective-permute-start.10 = (bf16[10,32,768]{2,1,0:T(8,128)(2,1)S(1)}, bf16[10,32,768]{2,1,0:T(8,128)(2,1)S(1)}, u32[]{:S(2)}, u32[]{:S(2)}) collective-permute-start(bf16[10,32,768]{2,1,0:T(8,128)(2,1)S(1)} %add_block.26), channel_id=1, source_target_pairs={{0,2},{1,3},{2,0},{3,1},{4,6},{5,7},{6,4},{7,5},{8,10},{9,11},{10,... | collective-permute-start | bytes 1474568 | tf_op jit(solution)/shard_map/ppermute | solution.py:624
  294.4 17.9 %collective-permute-start.14 = (bf16[10,32,768]{2,1,0:T(8,128)(2,1)S(1)}, bf16[10,32,768]{2,1,0:T(8,128)(2,1)S(1)}, u32[]{:S(2)}, u32[]{:S(2)}) collective-permute-start(bf16[10,32,768]{2,1,0:T(8,128)(2,1)S(1)} %add_block.29), channel_id=1, source_target_pairs={{0,1},{1,0},{2,3},{3,2},{4,5},{5,4},{6,7},{7,6},{8,9},{9,8},{10,11... | collective-permute-start | bytes 1474568 | tf_op jit(solution)/shard_map/ppermute | solution.py:624
  295.9 19.3 %collective-permute-start.15 = (bf16[10,32,768]{2,1,0:T(8,128)(2,1)S(1)}, bf16[10,32,768]{2,1,0:T(8,128)(2,1)S(1)}, u32[]{:S(2)}, u32[]{:S(2)}) collective-permute-start(bf16[10,32,768]{2,1,0:T(8,128)(2,1)S(1)} %add_block.30), channel_id=1, source_target_pairs={{0,2},{1,3},{2,0},{3,1},{4,6},{5,7},{6,4},{7,5},{8,10},{9,11},{10,... | collective-permute-start | bytes 1474568 | tf_op jit(solution)/shard_map/ppermute | solution.py:624
  302.0 13.2 %collective-permute-start.17 = (bf16[10,32,768]{2,1,0:T(8,128)(2,1)S(1)}, bf16[10,32,768]{2,1,0:T(8,128)(2,1)S(1)}, u32[]{:S(2)}, u32[]{:S(2)}) collective-permute-start(bf16[10,32,768]{2,1,0:T(8,128)(2,1)S(1)} %add_block.32), channel_id=1, source_target_pairs={{0,4},{1,5},{2,6},{3,7},{4,8},{5,9},{6,10},{7,11},{8,12},{9,13},{1... | collective-permute-start | bytes 1474568 | tf_op jit(solution)/shard_map/ppermute | solution.py:624
  304.1 14.9 %collective-permute-start.16 = (bf16[10,32,768]{2,1,0:T(8,128)(2,1)S(1)}, bf16[10,32,768]{2,1,0:T(8,128)(2,1)S(1)}, u32[]{:S(2)}, u32[]{:S(2)}) collective-permute-start(bf16[10,32,768]{2,1,0:T(8,128)(2,1)S(1)} %add_block.31), channel_id=1, source_target_pairs={{4,0},{5,1},{6,2},{7,3},{8,4},{9,5},{10,6},{11,7},{12,8},{13,9},{1... | collective-permute-start | bytes 1474568 | tf_op jit(solution)/shard_map/ppermute | solution.py:624
  305.4 6.0 %collective-permute-start.8 = (f32[12,768]{1,0:T(8,128)S(1)}, f32[12,768]{1,0:T(8,128)S(1)}, u32[]{:S(2)}, u32[]{:S(2)}) collective-permute-start(f32[12,768]{1,0:T(8,128)S(1)} %add.64), channel_id=1, source_target_pairs={{0,2},{1,3},{2,0},{3,1},{4,6},{5,7},{6,4},{7,5},{8,10},{9,11},{10,... | collective-permute-start | bytes 110600 | tf_op jit(solution)/shard_map/ppermute | solution.py:630
  313.0 12.2 %collective-permute-start.18 = (bf16[10,32,768]{2,1,0:T(8,128)(2,1)S(1)}, bf16[10,32,768]{2,1,0:T(8,128)(2,1)S(1)}, u32[]{:S(2)}, u32[]{:S(2)}) collective-permute-start(bf16[10,32,768]{2,1,0:T(8,128)(2,1)S(1)} %add_block.34), channel_id=1, source_target_pairs={{0,2},{1,3},{2,0},{3,1},{4,6},{5,7},{6,4},{7,5},{8,10},{9,11},{10,... | collective-permute-start | bytes 1474568 | tf_op jit(solution)/shard_map/ppermute | solution.py:624
  314.1 11.5 %collective-permute-start.23 = (bf16[10,32,768]{2,1,0:T(8,128)(2,1)S(1)}, bf16[10,32,768]{2,1,0:T(8,128)(2,1)S(1)}, u32[]{:S(2)}, u32[]{:S(2)}) collective-permute-start(bf16[10,32,768]{2,1,0:T(8,128)(2,1)S(1)} %add_block.33), channel_id=1, source_target_pairs={{0,1},{1,0},{2,3},{3,2},{4,5},{5,4},{6,7},{7,6},{8,9},{9,8},{10,11... | collective-permute-start | bytes 1474568 | tf_op jit(solution)/shard_map/ppermute | solution.py:624
  316.3 10.6 %collective-permute-start.20 = (bf16[10,32,768]{2,1,0:T(8,128)(2,1)S(1)}, bf16[10,32,768]{2,1,0:T(8,128)(2,1)S(1)}, u32[]{:S(2)}, u32[]{:S(2)}) collective-permute-start(bf16[10,32,768]{2,1,0:T(8,128)(2,1)S(1)} %add_block.36), channel_id=1, source_target_pairs={{0,4},{1,5},{2,6},{3,7},{4,8},{5,9},{6,10},{7,11},{8,12},{9,13},{1... | collective-permute-start | bytes 1474568 | tf_op jit(solution)/shard_map/ppermute | solution.py:624
  320.0 12.4 %collective-permute-start.19 = (bf16[10,32,768]{2,1,0:T(8,128)(2,1)S(1)}, bf16[10,32,768]{2,1,0:T(8,128)(2,1)S(1)}, u32[]{:S(2)}, u32[]{:S(2)}) collective-permute-start(bf16[10,32,768]{2,1,0:T(8,128)(2,1)S(1)} %add_block.35), channel_id=1, source_target_pairs={{4,0},{5,1},{6,2},{7,3},{8,4},{9,5},{10,6},{11,7},{12,8},{13,9},{1... | collective-permute-start | bytes 1474568 | tf_op jit(solution)/shard_map/ppermute | solution.py:624
  321.3 1.3 collective-permute-start.13
  322.6 15.3 %copy-start.5 = (f32[12,768]{1,0:T(8,128)}, f32[12,768]{1,0:T(8,128)S(1)}, u32[]{:S(2)}) copy-start(f32[12,768]{1,0:T(8,128)S(1)} %add.66) | copy-start | bytes 110596
  323.7 15.0 %collective-permute-start.22 = (bf16[10,32,768]{2,1,0:T(8,128)(2,1)S(1)}, bf16[10,32,768]{2,1,0:T(8,128)(2,1)S(1)}, u32[]{:S(2)}, u32[]{:S(2)}) collective-permute-start(bf16[10,32,768]{2,1,0:T(8,128)(2,1)S(1)} %add_block.38), channel_id=1, source_target_pairs={{0,2},{1,3},{2,0},{3,1},{4,6},{5,7},{6,4},{7,5},{8,10},{9,11},{10,... | collective-permute-start | bytes 1474568 | tf_op jit(solution)/shard_map/ppermute | solution.py:624
  327.9 13.5 %collective-permute-start.25 = (bf16[10,32,768]{2,1,0:T(8,128)(2,1)S(1)}, bf16[10,32,768]{2,1,0:T(8,128)(2,1)S(1)}, u32[]{:S(2)}, u32[]{:S(2)}) collective-permute-start(bf16[10,32,768]{2,1,0:T(8,128)(2,1)S(1)} %add_block.40), channel_id=1, source_target_pairs={{0,4},{1,5},{2,6},{3,7},{4,8},{5,9},{6,10},{7,11},{8,12},{9,13},{1... | collective-permute-start | bytes 1474568 | tf_op jit(solution)/shard_map/ppermute | solution.py:624
  333.4 13.5 %collective-permute-start.24 = (bf16[10,32,768]{2,1,0:T(8,128)(2,1)S(1)}, bf16[10,32,768]{2,1,0:T(8,128)(2,1)S(1)}, u32[]{:S(2)}, u32[]{:S(2)}) collective-permute-start(bf16[10,32,768]{2,1,0:T(8,128)(2,1)S(1)} %add_block.39), channel_id=1, source_target_pairs={{4,0},{5,1},{6,2},{7,3},{8,4},{9,5},{10,6},{11,7},{12,8},{13,9},{1... | collective-permute-start | bytes 1474568 | tf_op jit(solution)/shard_map/ppermute | solution.py:624
  335.9 11.3 %collective-permute-start.21 = (bf16[10,32,768]{2,1,0:T(8,128)(2,1)S(1)}, bf16[10,32,768]{2,1,0:T(8,128)(2,1)S(1)}, u32[]{:S(2)}, u32[]{:S(2)}) collective-permute-start(bf16[10,32,768]{2,1,0:T(8,128)(2,1)S(1)} %add_block.37), channel_id=1, source_target_pairs={{0,1},{1,0},{2,3},{3,2},{4,5},{5,4},{6,7},{7,6},{8,9},{9,8},{10,11... | collective-permute-start | bytes 1474568 | tf_op jit(solution)/shard_map/ppermute | solution.py:624
  338.6 9.8 %copy-start.1 = (f32[10,32,768]{2,1,0:T(8,128)S(1)}, f32[10,32,768]{2,1,0:T(8,128)}, u32[]{:S(2)}) copy-start(f32[10,32,768]{2,1,0:T(8,128)} %param.17) | copy-start | bytes 2949124
  338.6 9.8 %copy-start.2 = (f32[10,32,768]{2,1,0:T(8,128)S(1)}, f32[10,32,768]{2,1,0:T(8,128)}, u32[]{:S(2)}) copy-start(f32[10,32,768]{2,1,0:T(8,128)} %param.19) | copy-start | bytes 2949124
  338.6 9.8 %copy-start.3 = (f32[10,32,768]{2,1,0:T(8,128)S(1)}, f32[10,32,768]{2,1,0:T(8,128)}, u32[]{:S(2)}) copy-start(f32[10,32,768]{2,1,0:T(8,128)} %param.18) | copy-start | bytes 2949124
  (4 other events, 16.9 us)
Sparse Core Ops, SparseCore 0:
  11.5 112.7 all-gather.1

commit v2 on v1

--- a/solution.py
+++ b/solution.py
@@ -173,7 +173,7 @@
 
 ROWS = 512
 PAIRS_FWD = 2
-PAIRS_BWD = 1
+PAIRS_BWD = 2
 CHUNK = 1024
 
 

time: 359 us -> 358 us (level)
  no operation moved by 1% of the time
where the time goes in v2:
time: 358 us; the launch traced here: 356 us
  Pallas kernels  143 us (40%)
  waiting for transfers between devices  142 us (40%)
  starting transfers between devices  35.4 us (10%)
  between operations  15.3 us (4%)
  other arithmetic  10.6 us (3%)
  local copies, waits for them, and re-layouts  9.65 us (3%)
    all_gather x1, waiting for transfers between devices, local(): lax.all_gather(weight_slots.astype(BF), ('seq', 'batch'), axis=0, tiled=T...  110 us
    pallas_call x1, Pallas kernels, ffn(): pl.pallas_call(ffn_kernel, grid_spec=pltpu.PrefetchScalarGridSpec(num_sca...  48.3 us
    pallas_call x1, Pallas kernels, attn_bwd(): pl.pallas_call(attn_bwd_kernel, grid_spec=pltpu.PrefetchScalarGridSpec(nu...  38.8 us
    ppermute x20, starting transfers between devices, reduce_slots(): arrived[i] = lax.ppermute(give, 'batch', back)  30.6 us
    pallas_call x1, Pallas kernels, attn_fwd(): pl.pallas_call(attn_fwd_kernel, grid_spec=pltpu.PrefetchScalarGridSpec(nu...  29.9 us
    ppermute x20, waiting for transfers between devices, reduce_slots(): arrived[i] = lax.ppermute(give, 'batch', back)  20.3 us
    pallas_call x21, Pallas kernels, add_block(): pl.pallas_call(partial(add_kernel, tuple(flags)), grid_spec=pltpu.Prefetc...  17.6 us
    ppermute x3, waiting for transfers between devices, reduce_slots(): small = small + lax.ppermute(small, *steps.pop(0))  8.63 us
  transfers between devices with their start and end apart: 27, of which 15 were waited for; matrix products, arithmetic and copies ran while one was open for 4% of the time, Pallas kernels for 6%

profile of v2, /device:TPU:0, one launch (start us, length us, event | category | flops | bytes accessed | tf_op | source)
XLA Modules:
  0.0 356.4 jit_solution(13313932268694030082)
XLA Ops:
  7.2 2.0 convert_element_type.19
  12.9 1.9 select_add_fusion
  14.8 109.5 %all-gather.2.cloned.1.call-done.slots_ref.w_hbm = bf16[320,32,768]{2,1,0:T(8,128)(2,1)} async-done(((bf16[10,32,768]{2,1,0:T(8,128)(2,1)}), bf16[320,32,768]{2,1,0:T(8,128)(2,1)}) %all-gather.2.cloned.1.call-update) | async-done | bytes 15728656 | tf_op jit(solution)/shard_map/all_gather | solution.py:684
  124.3 29.9 %attn_fwd.1 = (bf16[2,512,768]{2,1,0:T(8,128)(2,1)}, bf16[2,512,768]{2,1,0:T(8,128)(2,1)}, bf16[2,512,768]{2,1,0:T(8,128)(2,1)}, bf16[2,512,768]{2,1,0:T(8,128)(...) custom-call(s32[2]{0:T(128)} %broadcast_subtract_fusion.limits, ...), custom_call_target="tpu_custom_call" | custom-call | tf_op jit(solution)/shard_map/attn_fwd/pallas_call | solution.py:153
  154.2 48.3 %ffn.1 = (bf16[1024,768]{1,0:T(8,128)(2,1)}, bf16[1024,768]{1,0:T(8,128)(2,1)}, f32[8,768]{1,0:T(8,128)}, f32[1,3072]{1,0:T(1,128)}, bf16[160,32,768]{2,1,0:T(8,128)(2,1)}, /*index=5*/bf16[160,32,768]{2,1,0:T(8,128)(2,1)}) custom-call(s32[288]{0:T(512)} %get-tuple-element.84.place, s32[288]{0:T(512)} %get-tuple-element.83.back, bf16[1024,768]{1,0:T(8,128)(2,1)} %bitcast.20, ...), custom_call_target="tpu_custom_call" | custom-call | tf_op jit(solution)/shard_map/ffn/pallas_call | solution.py:270
  202.5 38.8 %attn_bwd.1 = (f32[2,512,768]{2,1,0:T(8,128)}, f32[8,768]{1,0:T(8,128)}, bf16[160,32,768]{2,1,0:T(8,128)(2,1)}, bf16[160,32,768]{2,1,0:T(8,128)(2,1)}) custom-call(s32[2]{0:T(128)} %broadcast_subtract_fusion.limits, s32[288]{0:T(512)} %get-tuple-element.84.place, s32[288]{0:T(512)} %get-tuple-element.83.back, ...), custom_call_target="tpu_custom_call", output_to_operand_aliasing={{2}: (14, {}), {3}: (15, {})} | custom-call | tf_op jit(solution)/shard_map/attn_bwd/pallas_call | solution.py:375
  246.6 1.6 collective-permute-start.1
  248.9 3.6 %collective-permute-done.1 = f32[12,768]{1,0:T(8,128)S(1)} collective-permute-done((f32[12,768]{1,0:T(8,128)S(1)}, f32[12,768]{1,0:T(8,128)S(1)}, u32[]{:S(2)}, u32[]{:S(2)}) %collective-permute-start.1) | collective-permute-done | bytes 36896 | tf_op jit(solution)/shard_map/ppermute | solution.py:612
  252.7 3.2 copy-done
  255.9 5.3 %load_core.1.mine = bf16[16,10,32,768]{3,2,1,0:T(8,128)(2,1)S(1)} custom-call(bf16[16,10,32,768]{3,2,1,0:T(8,128)(2,1)S(1)} %bitcast.17), custom_call_target="tpu_custom_call" | custom-call | bytes 15728640 | tf_op jit(solution)/shard_map/load_core/pallas_call | solution.py:516
  261.3 3.5 add_cores.1.own
  265.4 3.3 collective-permute-start.4
  269.4 1.3 collective-permute-start.7
  272.8 1.5 collective-permute-start.3
  274.2 2.6 collective-permute-start.5
  278.8 2.7 collective-permute-done.3
  281.5 1.3 collective-permute-start.12
  284.3 1.5 collective-permute-start.9
  286.5 3.0 collective-permute-done.5.refs_0_
  290.1 2.7 collective-permute-done.12.refs_1_
  293.6 1.5 collective-permute-start.14
  295.7 2.8 collective-permute-done.9.refs_0_
  298.5 1.5 collective-permute-done.10.refs_1_
  301.0 1.3 collective-permute-start.17
  303.2 1.3 collective-permute-start.16
  305.8 4.7 %collective-permute-done.8 = f32[12,768]{1,0:T(8,128)S(1)} collective-permute-done((f32[12,768]{1,0:T(8,128)S(1)}, f32[12,768]{1,0:T(8,128)S(1)}, u32[]{:S(2)}, u32[]{:S(2)}) %collective-permute-start.8) | collective-permute-done | bytes 36896 | tf_op jit(solution)/shard_map/ppermute | solution.py:630
  315.3 2.7 collective-permute-start.20
  327.0 4.5 %collective-permute-start.25 = (bf16[10,32,768]{2,1,0:T(8,128)(2,1)S(1)}, bf16[10,32,768]{2,1,0:T(8,128)(2,1)S(1)}, u32[]{:S(2)}, u32[]{:S(2)}) collective-permute-start(bf16[10,32,768]{2,1,0:T(8,128)(2,1)S(1)} %add_block.40), channel_id=1, source_target_pairs={{0,4},{1,5},{2,6},{3,7},{4,8},{5,9},{6,10},{7,11},{8,12},{9,13},{1... | collective-permute-start | bytes 1474568 | tf_op jit(solution)/shard_map/ppermute | solution.py:624
  332.5 1.4 collective-permute-start.24
  337.8 2.4 collective-permute-done.25.refs_3_
  340.2 5.6 %collective-permute-done.24.refs_2_ = bf16[10,32,768]{2,1,0:T(8,128)(2,1)S(1)} collective-permute-done((bf16[10,32,768]{2,1,0:T(8,128)(2,1)S(1)}, bf16[10,32,768]{2,1,0:T(8,128)(2,1)S(1)}, u32[]{:S(2)}, u32[]{:S(2)}) %collective-permute-start.24) | collective-permute-done | bytes 491552 | tf_op jit(solution)/shard_map/ppermute | solution.py:624
  347.3 2.3 multiply_subtract_fusion
  (94 shorter events, 41.6 us)
Async XLA Ops:
  7.2 117.1 %all-gather.2.cloned.1.call-start = ((), (), s32[]{:S(2)}) async-start(), calls=%async_computation | async-start | bytes 16220160 | tf_op jit(solution)/shard_map/all_gather | solution.py:684
  202.5 43.4 %copy-start.8 = (f32[1,3072]{1,0:T(1,128)S(1)}, f32[1,3072]{1,0:T(1,128)}, u32[]{:S(2)}) copy-start(f32[1,3072]{1,0:T(1,128)} %get-tuple-element.60) | copy-start | bytes 36868
  241.3 20.0 %collective-permute-start = (bf16[160,32,768]{2,1,0:T(8,128)(2,1)}, bf16[160,32,768]{2,1,0:T(8,128)(2,1)}, u32[]{:S(2)}, u32[]{:S(2)}) collective-permute-start(bf16[160,32,768]{2,1,0:T(8,128)(2,1)} %get-tuple-element.57), channel_id=1, source_target_pairs={{0,16},{16,0},{1,17},{17,1},{2,18},{18,2},{3,19},{19,3},{4,20},{20... | collective-permute-start | bytes 23592968 | tf_op jit(solution)/shard_map/ppermute | solution.py:606
  246.6 5.9 %collective-permute-start.1 = (f32[12,768]{1,0:T(8,128)S(1)}, f32[12,768]{1,0:T(8,128)S(1)}, u32[]{:S(2)}, u32[]{:S(2)}) collective-permute-start(f32[12,768]{1,0:T(8,128)S(1)} %concatenate.7), channel_id=1, source_target_pairs={{0,8},{1,9},{2,10},{3,11},{4,12},{5,13},{6,14},{7,15},{8,0},{9,1},... | collective-permute-start | bytes 110600 | tf_op jit(solution)/shard_map/ppermute | solution.py:612
  252.5 8.7 %collective-permute-start.2 = (f32[12,768]{1,0:T(8,128)S(1)}, f32[12,768]{1,0:T(8,128)S(1)}, u32[]{:S(2)}, u32[]{:S(2)}) collective-permute-start(f32[12,768]{1,0:T(8,128)S(1)} %add.62), channel_id=1, source_target_pairs={{0,4},{1,5},{2,6},{3,7},{4,0},{5,1},{6,2},{7,3},{8,12},{9,13},{10,... | collective-permute-start | bytes 110600 | tf_op jit(solution)/shard_map/ppermute | solution.py:612
  265.4 17.4 %collective-permute-start.4 = (bf16[10,32,768]{2,1,0:T(8,128)(2,1)S(1)}, bf16[10,32,768]{2,1,0:T(8,128)(2,1)S(1)}, u32[]{:S(2)}, u32[]{:S(2)}) collective-permute-start(bf16[10,32,768]{2,1,0:T(8,128)(2,1)S(1)} %add_block.21), channel_id=1, source_target_pairs={{0,1},{1,0},{2,3},{3,2},{12,13},{13,12},{14,15},{15,14},{16,17},{1... | collective-permute-start | bytes 1474568 | tf_op jit(solution)/shard_map/ppermute | solution.py:624
  269.4 14.9 %collective-permute-start.7 = (bf16[10,32,768]{2,1,0:T(8,128)(2,1)S(1)}, bf16[10,32,768]{2,1,0:T(8,128)(2,1)S(1)}, u32[]{:S(2)}, u32[]{:S(2)}) collective-permute-start(bf16[10,32,768]{2,1,0:T(8,128)(2,1)S(1)} %add_block.24), channel_id=1, source_target_pairs={{0,4},{1,5},{2,6},{3,7},{16,20},{17,21},{18,22},{19,23}} | collective-permute-start | bytes 1474568 | tf_op jit(solution)/shard_map/ppermute | solution.py:624
  271.4 14.4 %collective-permute-start.6 = (bf16[10,32,768]{2,1,0:T(8,128)(2,1)S(1)}, bf16[10,32,768]{2,1,0:T(8,128)(2,1)S(1)}, u32[]{:S(2)}, u32[]{:S(2)}) collective-permute-start(bf16[10,32,768]{2,1,0:T(8,128)(2,1)S(1)} %add_block.23), channel_id=1, source_target_pairs={{12,8},{13,9},{14,10},{15,11},{28,24},{29,25},{30,26},{31,27}} | collective-permute-start | bytes 1474568 | tf_op jit(solution)/shard_map/ppermute | solution.py:624
  272.8 8.7 %collective-permute-start.3 = (f32[12,768]{1,0:T(8,128)S(1)}, f32[12,768]{1,0:T(8,128)S(1)}, u32[]{:S(2)}, u32[]{:S(2)}) collective-permute-start(f32[12,768]{1,0:T(8,128)S(1)} %add.63), channel_id=1, source_target_pairs={{0,1},{1,0},{2,3},{3,2},{4,5},{5,4},{6,7},{7,6},{8,9},{9,8},{10,11... | collective-permute-start | bytes 110600 | tf_op jit(solution)/shard_map/ppermute | solution.py:630
  274.2 15.2 %collective-permute-start.5 = (bf16[10,32,768]{2,1,0:T(8,128)(2,1)S(1)}, bf16[10,32,768]{2,1,0:T(8,128)(2,1)S(1)}, u32[]{:S(2)}, u32[]{:S(2)}) collective-permute-start(bf16[10,32,768]{2,1,0:T(8,128)(2,1)S(1)} %add_block.22), channel_id=1, source_target_pairs={{0,2},{1,3},{2,0},{3,1},{12,14},{13,15},{14,12},{15,13},{16,18},{1... | collective-permute-start | bytes 1474568 | tf_op jit(solution)/shard_map/ppermute | solution.py:624
  281.5 11.3 %collective-permute-start.12 = (bf16[10,32,768]{2,1,0:T(8,128)(2,1)S(1)}, bf16[10,32,768]{2,1,0:T(8,128)(2,1)S(1)}, u32[]{:S(2)}, u32[]{:S(2)}) collective-permute-start(bf16[10,32,768]{2,1,0:T(8,128)(2,1)S(1)} %add_block.28), channel_id=1, source_target_pairs={{0,4},{1,5},{2,6},{3,7},{4,8},{5,9},{6,10},{7,11},{16,20},{17,21},... | collective-permute-start | bytes 1474568 | tf_op jit(solution)/shard_map/ppermute | solution.py:624
  282.8 10.0 %collective-permute-start.11 = (bf16[10,32,768]{2,1,0:T(8,128)(2,1)S(1)}, bf16[10,32,768]{2,1,0:T(8,128)(2,1)S(1)}, u32[]{:S(2)}, u32[]{:S(2)}) collective-permute-start(bf16[10,32,768]{2,1,0:T(8,128)(2,1)S(1)} %add_block.27), channel_id=1, source_target_pairs={{8,4},{9,5},{10,6},{11,7},{12,8},{13,9},{14,10},{15,11},{24,20},{2... | collective-permute-start | bytes 1474568 | tf_op jit(solution)/shard_map/ppermute | solution.py:624
  284.3 14.1 %collective-permute-start.9 = (bf16[10,32,768]{2,1,0:T(8,128)(2,1)S(1)}, bf16[10,32,768]{2,1,0:T(8,128)(2,1)S(1)}, u32[]{:S(2)}, u32[]{:S(2)}) collective-permute-start(bf16[10,32,768]{2,1,0:T(8,128)(2,1)S(1)} %add_block.25), channel_id=1, source_target_pairs={{0,1},{1,0},{2,3},{3,2},{4,5},{5,4},{6,7},{7,6},{8,9},{9,8},{10,11... | collective-permute-start | bytes 1474568 | tf_op jit(solution)/shard_map/ppermute | solution.py:624
  285.8 14.2 %collective-permute-start.10 = (bf16[10,32,768]{2,1,0:T(8,128)(2,1)S(1)}, bf16[10,32,768]{2,1,0:T(8,128)(2,1)S(1)}, u32[]{:S(2)}, u32[]{:S(2)}) collective-permute-start(bf16[10,32,768]{2,1,0:T(8,128)(2,1)S(1)} %add_block.26), channel_id=1, source_target_pairs={{0,2},{1,3},{2,0},{3,1},{4,6},{5,7},{6,4},{7,5},{8,10},{9,11},{10,... | collective-permute-start | bytes 1474568 | tf_op jit(solution)/shard_map/ppermute | solution.py:624
  293.6 17.7 %collective-permute-start.14 = (bf16[10,32,768]{2,1,0:T(8,128)(2,1)S(1)}, bf16[10,32,768]{2,1,0:T(8,128)(2,1)S(1)}, u32[]{:S(2)}, u32[]{:S(2)}) collective-permute-start(bf16[10,32,768]{2,1,0:T(8,128)(2,1)S(1)} %add_block.29), channel_id=1, source_target_pairs={{0,1},{1,0},{2,3},{3,2},{4,5},{5,4},{6,7},{7,6},{8,9},{9,8},{10,11... | collective-permute-start | bytes 1474568 | tf_op jit(solution)/shard_map/ppermute | solution.py:624
  295.1 19.2 %collective-permute-start.15 = (bf16[10,32,768]{2,1,0:T(8,128)(2,1)S(1)}, bf16[10,32,768]{2,1,0:T(8,128)(2,1)S(1)}, u32[]{:S(2)}, u32[]{:S(2)}) collective-permute-start(bf16[10,32,768]{2,1,0:T(8,128)(2,1)S(1)} %add_block.30), channel_id=1, source_target_pairs={{0,2},{1,3},{2,0},{3,1},{4,6},{5,7},{6,4},{7,5},{8,10},{9,11},{10,... | collective-permute-start | bytes 1474568 | tf_op jit(solution)/shard_map/ppermute | solution.py:624
  301.0 13.3 %collective-permute-start.17 = (bf16[10,32,768]{2,1,0:T(8,128)(2,1)S(1)}, bf16[10,32,768]{2,1,0:T(8,128)(2,1)S(1)}, u32[]{:S(2)}, u32[]{:S(2)}) collective-permute-start(bf16[10,32,768]{2,1,0:T(8,128)(2,1)S(1)} %add_block.32), channel_id=1, source_target_pairs={{0,4},{1,5},{2,6},{3,7},{4,8},{5,9},{6,10},{7,11},{8,12},{9,13},{1... | collective-permute-start | bytes 1474568 | tf_op jit(solution)/shard_map/ppermute | solution.py:624
  303.2 14.9 %collective-permute-start.16 = (bf16[10,32,768]{2,1,0:T(8,128)(2,1)S(1)}, bf16[10,32,768]{2,1,0:T(8,128)(2,1)S(1)}, u32[]{:S(2)}, u32[]{:S(2)}) collective-permute-start(bf16[10,32,768]{2,1,0:T(8,128)(2,1)S(1)} %add_block.31), channel_id=1, source_target_pairs={{4,0},{5,1},{6,2},{7,3},{8,4},{9,5},{10,6},{11,7},{12,8},{13,9},{1... | collective-permute-start | bytes 1474568 | tf_op jit(solution)/shard_map/ppermute | solution.py:624
  304.5 6.0 %collective-permute-start.8 = (f32[12,768]{1,0:T(8,128)S(1)}, f32[12,768]{1,0:T(8,128)S(1)}, u32[]{:S(2)}, u32[]{:S(2)}) collective-permute-start(f32[12,768]{1,0:T(8,128)S(1)} %add.64), channel_id=1, source_target_pairs={{0,2},{1,3},{2,0},{3,1},{4,6},{5,7},{6,4},{7,5},{8,10},{9,11},{10,... | collective-permute-start | bytes 110600 | tf_op jit(solution)/shard_map/ppermute | solution.py:630
  312.1 12.2 %collective-permute-start.18 = (bf16[10,32,768]{2,1,0:T(8,128)(2,1)S(1)}, bf16[10,32,768]{2,1,0:T(8,128)(2,1)S(1)}, u32[]{:S(2)}, u32[]{:S(2)}) collective-permute-start(bf16[10,32,768]{2,1,0:T(8,128)(2,1)S(1)} %add_block.34), channel_id=1, source_target_pairs={{0,2},{1,3},{2,0},{3,1},{4,6},{5,7},{6,4},{7,5},{8,10},{9,11},{10,... | collective-permute-start | bytes 1474568 | tf_op jit(solution)/shard_map/ppermute | solution.py:624
  313.1 11.6 %collective-permute-start.23 = (bf16[10,32,768]{2,1,0:T(8,128)(2,1)S(1)}, bf16[10,32,768]{2,1,0:T(8,128)(2,1)S(1)}, u32[]{:S(2)}, u32[]{:S(2)}) collective-permute-start(bf16[10,32,768]{2,1,0:T(8,128)(2,1)S(1)} %add_block.33), channel_id=1, source_target_pairs={{0,1},{1,0},{2,3},{3,2},{4,5},{5,4},{6,7},{7,6},{8,9},{9,8},{10,11... | collective-permute-start | bytes 1474568 | tf_op jit(solution)/shard_map/ppermute | solution.py:624
  315.3 10.7 %collective-permute-start.20 = (bf16[10,32,768]{2,1,0:T(8,128)(2,1)S(1)}, bf16[10,32,768]{2,1,0:T(8,128)(2,1)S(1)}, u32[]{:S(2)}, u32[]{:S(2)}) collective-permute-start(bf16[10,32,768]{2,1,0:T(8,128)(2,1)S(1)} %add_block.36), channel_id=1, source_target_pairs={{0,4},{1,5},{2,6},{3,7},{4,8},{5,9},{6,10},{7,11},{8,12},{9,13},{1... | collective-permute-start | bytes 1474568 | tf_op jit(solution)/shard_map/ppermute | solution.py:624
  319.0 12.6 %collective-permute-start.19 = (bf16[10,32,768]{2,1,0:T(8,128)(2,1)S(1)}, bf16[10,32,768]{2,1,0:T(8,128)(2,1)S(1)}, u32[]{:S(2)}, u32[]{:S(2)}) collective-permute-start(bf16[10,32,768]{2,1,0:T(8,128)(2,1)S(1)} %add_block.35), channel_id=1, source_target_pairs={{4,0},{5,1},{6,2},{7,3},{8,4},{9,5},{10,6},{11,7},{12,8},{13,9},{1... | collective-permute-start | bytes 1474568 | tf_op jit(solution)/shard_map/ppermute | solution.py:624
  320.3 1.3 collective-permute-start.13
  321.6 15.5 %copy-start.5 = (f32[12,768]{1,0:T(8,128)}, f32[12,768]{1,0:T(8,128)S(1)}, u32[]{:S(2)}) copy-start(f32[12,768]{1,0:T(8,128)S(1)} %add.66) | copy-start | bytes 110596
  322.7 15.1 %collective-permute-start.22 = (bf16[10,32,768]{2,1,0:T(8,128)(2,1)S(1)}, bf16[10,32,768]{2,1,0:T(8,128)(2,1)S(1)}, u32[]{:S(2)}, u32[]{:S(2)}) collective-permute-start(bf16[10,32,768]{2,1,0:T(8,128)(2,1)S(1)} %add_block.38), channel_id=1, source_target_pairs={{0,2},{1,3},{2,0},{3,1},{4,6},{5,7},{6,4},{7,5},{8,10},{9,11},{10,... | collective-permute-start | bytes 1474568 | tf_op jit(solution)/shard_map/ppermute | solution.py:624
  327.0 13.2 %collective-permute-start.25 = (bf16[10,32,768]{2,1,0:T(8,128)(2,1)S(1)}, bf16[10,32,768]{2,1,0:T(8,128)(2,1)S(1)}, u32[]{:S(2)}, u32[]{:S(2)}) collective-permute-start(bf16[10,32,768]{2,1,0:T(8,128)(2,1)S(1)} %add_block.40), channel_id=1, source_target_pairs={{0,4},{1,5},{2,6},{3,7},{4,8},{5,9},{6,10},{7,11},{8,12},{9,13},{1... | collective-permute-start | bytes 1474568 | tf_op jit(solution)/shard_map/ppermute | solution.py:624
  332.5 13.3 %collective-permute-start.24 = (bf16[10,32,768]{2,1,0:T(8,128)(2,1)S(1)}, bf16[10,32,768]{2,1,0:T(8,128)(2,1)S(1)}, u32[]{:S(2)}, u32[]{:S(2)}) collective-permute-start(bf16[10,32,768]{2,1,0:T(8,128)(2,1)S(1)} %add_block.39), channel_id=1, source_target_pairs={{4,0},{5,1},{6,2},{7,3},{8,4},{9,5},{10,6},{11,7},{12,8},{13,9},{1... | collective-permute-start | bytes 1474568 | tf_op jit(solution)/shard_map/ppermute | solution.py:624
  335.0 11.0 %collective-permute-start.21 = (bf16[10,32,768]{2,1,0:T(8,128)(2,1)S(1)}, bf16[10,32,768]{2,1,0:T(8,128)(2,1)S(1)}, u32[]{:S(2)}, u32[]{:S(2)}) collective-permute-start(bf16[10,32,768]{2,1,0:T(8,128)(2,1)S(1)} %add_block.37), channel_id=1, source_target_pairs={{0,1},{1,0},{2,3},{3,2},{4,5},{5,4},{6,7},{7,6},{8,9},{9,8},{10,11... | collective-permute-start | bytes 1474568 | tf_op jit(solution)/shard_map/ppermute | solution.py:624
  337.8 9.4 %copy-start.1 = (f32[10,32,768]{2,1,0:T(8,128)S(1)}, f32[10,32,768]{2,1,0:T(8,128)}, u32[]{:S(2)}) copy-start(f32[10,32,768]{2,1,0:T(8,128)} %param.17) | copy-start | bytes 2949124
  337.8 9.4 %copy-start.2 = (f32[10,32,768]{2,1,0:T(8,128)S(1)}, f32[10,32,768]{2,1,0:T(8,128)}, u32[]{:S(2)}) copy-start(f32[10,32,768]{2,1,0:T(8,128)} %param.19) | copy-start | bytes 2949124
  337.8 9.4 %copy-start.3 = (f32[10,32,768]{2,1,0:T(8,128)S(1)}, f32[10,32,768]{2,1,0:T(8,128)}, u32[]{:S(2)}) copy-start(f32[10,32,768]{2,1,0:T(8,128)} %param.18) | copy-start | bytes 2949124
  (4 other events, 17.1 us)
Sparse Core Ops, SparseCore 0:
  11.5 112.7 all-gather.1
